TPU v7x, 128 devices: a whole 4x4x4 slice. The times are simulated.
128 devices in a mesh: visit: 4 (over y), patch: 32 (over x, z, core).
Axes of the slice: x: 4, y: 4, z: 4, core: 2. Of those that a mesh axis runs over, the one named last changes fastest.
Arguments:
- image: float32 [4, 32, 32, 128, 128], P('visit', 'patch'), may hold values from -6 to 6
- variance: float32 [4, 32, 32, 128, 128], P('visit', 'patch'), may hold values from 4 to 64
- dest_patch: int32 [4, 32, 32], P('visit', 'patch'), may hold values from 0 to 31, as said below
- quadrant: int32 [4, 32, 32], P('visit', 'patch'), may hold values from 0 to 3
- coef_index: int32 [4, 32, 32], P('visit', 'patch'), may hold values from 0 to 799
- block_count: int32 [4, 32], P('visit', 'patch'), may hold values from 24 to 32, as said below
- coef_table: float32 [800, 16, 6], replicated, may hold values from -0.625 to 0.625
- row_taps: float32 [16, 41], replicated, may hold values from -1 to 1
- col_taps: float32 [16, 41], replicated, may hold values from -1 to 1
Outputs:
- weighted_sum: float32 [32, 256, 256], P('patch', 'visit')
- weight_sum: float32 [32, 256, 256], P('patch', 'visit')
Inputs may be any that keep to these rules, and one draw needn't show every extreme that they name: `dest_patch`: among the blocks of one device at most 2 name the same patch slice; one patch slice, drawn from the seed, is named by exactly 2 live blocks of every device. `block_count`: some device has all 32 blocks live.
All inputs are finite; a program needn't handle non-finite values.
Results may differ from a plain program's by a relative error of at most 0.0003.
Values sent between devices are 32-bit elements; how exact they have to be, the bound alone decides.
A program may use at most 192 MiB of HBM per device.

v0:
```python
import jax
import jax.numpy as jnp
from jax import lax
from jax.sharding import PartitionSpec as P

highest = lax.Precision.HIGHEST


def band_matrices(filter_taps, block_side, reversed_band):
    radius = (filter_taps.shape[1] - 1) // 2
    row_index = jnp.arange(block_side)[:, None]
    col_index = jnp.arange(block_side)[None, :]
    offset = row_index - col_index if reversed_band else col_index - row_index
    banded = jnp.zeros((filter_taps.shape[0], block_side, block_side), jnp.float32)
    for tap_index in range(filter_taps.shape[1]):
        picked = (offset == tap_index - radius).astype(jnp.float32)
        banded = banded + filter_taps[:, tap_index, None, None] * picked[None, :, :]
    return banded


def match_blocks(pixels, coefficients, down_quarter, across_quarter, row_band, col_band):
    block_side = pixels.shape[-1]
    pixel_index = jnp.arange(block_side).astype(jnp.float32)
    across_pos = (
        across_quarter[:, None] * block_side + pixel_index[None, :] + 0.5
    ) / block_side - 1.0
    down_pos = (down_quarter[:, None] * block_side + pixel_index[None, :] + 0.5) / block_side - 1.0
    across_pos = across_pos[:, None, :]
    down_pos = down_pos[:, :, None]
    matched = jnp.zeros(pixels.shape, jnp.float32)
    for basis_index in range(row_band.shape[0]):
        spread = jnp.einsum(
            "nij,jk->nik",
            pixels,
            row_band[basis_index],
            precision=highest,
            preferred_element_type=jnp.float32,
        )
        convolved = jnp.einsum(
            "ij,njk->nik",
            col_band[basis_index],
            spread,
            precision=highest,
            preferred_element_type=jnp.float32,
        )
        poly_terms = coefficients[:, basis_index, :]
        weight = (
            poly_terms[:, 0, None, None]
            + poly_terms[:, 1, None, None] * across_pos
            + poly_terms[:, 2, None, None] * down_pos
            + poly_terms[:, 3, None, None] * across_pos * across_pos
            + poly_terms[:, 4, None, None] * across_pos * down_pos
            + poly_terms[:, 5, None, None] * down_pos * down_pos
        )
        matched = matched + weight * convolved
    return matched


def on_device(
    image, variance, dest_patch, quadrant, coef_index, block_count, coef_table, row_taps, col_taps
):
    pixels = image[0, 0]
    variances = variance[0, 0]
    targets = dest_patch[0, 0]
    quadrants = quadrant[0, 0]
    table_rows = coef_index[0, 0]
    live_count = block_count[0, 0]
    blocks = pixels.shape[0]
    block_side = pixels.shape[-1]
    owners = lax.axis_size("patch")
    capacity = max(2, (2 * blocks + owners - 1) // owners)
    slot_total = owners * capacity
    position = jnp.arange(blocks)
    is_live = position < live_count
    earlier_same = (
        (targets[:, None] == targets[None, :])
        & is_live[None, :]
        & (position[None, :] < position[:, None])
    )
    slot_rank = jnp.sum(earlier_same.astype(jnp.int32), axis=1)
    slot_of = jnp.where(is_live, targets * capacity + slot_rank, -1)
    slot_match = slot_of[None, :] == jnp.arange(slot_total)[:, None]
    occupied = jnp.any(slot_match, axis=1)
    source = jnp.sum(slot_match.astype(jnp.int32) * position[None, :], axis=1)
    presence = occupied.astype(jnp.float32)
    quarter_hot = (quadrants[:, None] == jnp.arange(4)[None, :]).astype(jnp.float32)
    slot_quarter = (jnp.take(quarter_hot, source, axis=0) * presence[:, None]).reshape(
        owners, capacity, 4
    )
    row_band = band_matrices(row_taps, block_side, False)
    col_band = band_matrices(col_taps, block_side, True)
    grid_shape = (owners, capacity, block_side, block_side)
    slot_pixels = (jnp.take(pixels, source, axis=0) * presence[:, None, None]).reshape(grid_shape)
    slot_variance = jnp.where(
        occupied[:, None, None], jnp.take(variances, source, axis=0), 1.0
    ).reshape(grid_shape)
    slot_coefficients = (
        jnp.take(coef_table, jnp.take(table_rows, source), axis=0) * presence[:, None, None]
    ).reshape((owners, capacity) + coef_table.shape[1:])
    got_pixels = lax.all_to_all(slot_pixels, "patch", split_axis=0, concat_axis=0, tiled=True)
    got_variance = lax.all_to_all(slot_variance, "patch", split_axis=0, concat_axis=0, tiled=True)
    got_coefficients = lax.all_to_all(
        slot_coefficients, "patch", split_axis=0, concat_axis=0, tiled=True
    )
    got_quarter = lax.all_to_all(slot_quarter, "patch", split_axis=0, concat_axis=0, tiled=True)
    senders = got_pixels.shape[0]
    items = got_pixels.shape[1]
    flat_quarter = got_quarter.reshape(senders * items, 4)
    matched = match_blocks(
        got_pixels.reshape(senders * items, block_side, block_side),
        got_coefficients.reshape((senders * items,) + got_coefficients.shape[2:]),
        flat_quarter[:, 2] + flat_quarter[:, 3],
        flat_quarter[:, 1] + flat_quarter[:, 3],
        row_band,
        col_band,
    )
    inverse = jnp.sum(flat_quarter, axis=1)[:, None, None] / got_variance.reshape(
        senders * items, block_side, block_side
    )
    weighted_slots, inverse_slots, got_quarter = (
        (inverse * matched).reshape(got_pixels.shape),
        inverse.reshape(got_pixels.shape),
        got_quarter,
    )
    quarter_grid = got_quarter.reshape(-1, 2, 2)
    weighted_patch = jnp.einsum(
        "nab,nij->aibj",
        quarter_grid,
        weighted_slots.reshape(-1, block_side, block_side),
        precision=highest,
        preferred_element_type=jnp.float32,
    ).reshape(2 * block_side, 2 * block_side)
    weight_patch = jnp.einsum(
        "nab,nij->aibj",
        quarter_grid,
        inverse_slots.reshape(-1, block_side, block_side),
        precision=highest,
        preferred_element_type=jnp.float32,
    ).reshape(2 * block_side, 2 * block_side)
    weighted_sum, weight_sum = (
        lax.psum_scatter(weighted_patch, "visit", scatter_dimension=0, tiled=True),
        lax.psum_scatter(weight_patch, "visit", scatter_dimension=0, tiled=True),
    )
    return (weighted_sum[None], weight_sum[None])


def solution(mesh):
    placed = (
        P("visit", "patch", None, None, None),
        P("visit", "patch", None, None, None),
        P("visit", "patch", None),
        P("visit", "patch", None),
        P("visit", "patch", None),
        P("visit", "patch"),
        P(),
        P(),
        P(),
    )
    return jax.shard_map(
        on_device,
        mesh=mesh,
        in_specs=placed,
        out_specs=(P("patch", "visit", None), P("patch", "visit", None)),
        check_vma=False,
    )
```

profile of v0, /device:TPU:0, one launch (start us, length us, event | category | flops | bytes accessed | tf_op | source)
XLA Modules:
  0.0 489.0 jit_solution(8101281087806809935)
XLA Ops:
  13.7 8.2 %all-to-all-start = ((f32[32,2,4]{2,1,0:T(2,128)}), f32[32,2,4]{2,1,0:T(2,128)S(1)}, u32[]{:S(2)}, u32[]{:S(2)}) async-start(f32[32,2,4]{2,1,0:T(2,128)} %select_multiply_fusion.2), calls=%async_computation | async-start | bytes 65536 | tf_op jit(solution)/shard_map/all_to_all | solution.py:105
  68.3 6.3 %select_select_fusion = (f32[64,128,128]{2,1,0:T(8,128)}, f32[64,128,128]{2,1,0:T(8,128)}) fusion(f32[64,128,128]{2,1,0:T(8,128)} %gather_fusion.3, pred[64]{0:T(512)(128)(4,1)} %compare_and_fusion.2, pred[64]{0:T(512)(128)(4,1)} %copy-done.92, f32[64]{0:T(128)S(1)} %convert_element_type.695, f32[64,128,128]{2,1,0:T(8,128)} %gather_fusion.4), kind=kLoop, calls=%fused_computation.40 | loop fusion | flops 4194304 | bytes 16777600 | tf_op jit(solution)/shard_map/jit(_where)/select_n | solution.py:94
  80.5 7.4 %all-to-all-start.2 = ((f32[32,1,192]{2,1,0:T(1,128)}), f32[32,1,192]{2,1,0:T(1,128)S(1)}, u32[]{:S(2)}, u32[]{:S(2)}) async-start(f32[32,1,192]{2,1,0:T(1,128)} %reshape.5191), calls=%async_computation.2 | async-start | bytes 65536 | tf_op jit(solution)/shard_map/all_to_all | solution.py:102
  87.9 5.6 %copy.170 = f32[32,2,128,128]{2,3,1,0:T(8,128)} copy(f32[32,2,128,128]{3,2,1,0:T(8,128)} %bitcast.540) | data formatting | bytes 8388608 | tf_op jit(solution)/shard_map/reshape | solution.py:96
  95.4 6.3 %all-to-all-start.3 = ((f32[32,2,128,128]{3,2,1,0:T(8,128)}), f32[32,2,128,128]{3,2,1,0:T(8,128)}, u32[]{:S(2)}, u32[]{:S(2)}) async-start(f32[32,2,128,128]{3,2,1,0:T(8,128)} %bitcast.539), calls=%async_computation.3 | async-start | bytes 8388608 | tf_op jit(solution)/shard_map/all_to_all | solution.py:100
  114.0 40.5 %all-to-all-done.3 = f32[32,2,128,128]{3,2,1,0:T(8,128)} async-done(((f32[32,2,128,128]{3,2,1,0:T(8,128)}), f32[32,2,128,128]{3,2,1,0:T(8,128)}, u32[]{:S(2)}, u32[]{:S(2)}) %all-to-all-start.3) | async-done | bytes 4194336 | tf_op jit(solution)/shard_map/all_to_all | solution.py:100
  154.5 6.6 %all-to-all-start.1 = ((f32[32,2,128,128]{2,3,1,0:T(8,128)}), f32[32,2,128,128]{2,3,1,0:T(8,128)}, u32[]{:S(2)}, u32[]{:S(2)}) async-start(f32[32,2,128,128]{2,3,1,0:T(8,128)} %copy.170), calls=%async_computation.1 | async-start | bytes 8388608 | tf_op jit(solution)/shard_map/all_to_all | solution.py:101
  161.4 8.0 %fusion.19 = f32[64,128,128]{1,2,0:T(8,128)} fusion(f32[64,128,128]{2,1,0:T(8,128)} %bitcast.23, f32[16,128,128]{2,1,0:T(8,128)S(1)} %multiply_add_fusion.1), kind=kOutput, calls=%fused_computation.71 | convolution fusion | flops 1610612736 | bytes 8454144 | tf_op jit(solution)/shard_map/nij,jk->nik/dot_general | solution.py:32
  169.4 8.0 %fusion.21 = f32[64,128,128]{1,2,0:T(8,128)} fusion(f32[64,128,128]{2,1,0:T(8,128)} %bitcast.23, f32[16,128,128]{2,1,0:T(8,128)S(1)} %multiply_add_fusion.1), kind=kOutput, calls=%fused_computation.75 | convolution fusion | flops 1610612736 | bytes 8454144 | tf_op jit(solution)/shard_map/nij,jk->nik/dot_general | solution.py:32
  177.4 8.1 %fusion.23 = f32[64,128,128]{1,2,0:T(8,128)} fusion(f32[64,128,128]{2,1,0:T(8,128)} %bitcast.23, f32[16,128,128]{2,1,0:T(8,128)S(1)} %multiply_add_fusion.1), kind=kOutput, calls=%fused_computation.79 | convolution fusion | flops 1610612736 | bytes 8454144 | tf_op jit(solution)/shard_map/nij,jk->nik/dot_general | solution.py:32
  185.5 8.3 %fusion.25 = f32[64,128,128]{1,2,0:T(8,128)} fusion(f32[64,128,128]{2,1,0:T(8,128)} %bitcast.23, f32[16,128,128]{2,1,0:T(8,128)S(1)} %multiply_add_fusion.1), kind=kOutput, calls=%fused_computation.83 | convolution fusion | flops 1610612736 | bytes 8454144 | tf_op jit(solution)/shard_map/nij,jk->nik/dot_general | solution.py:32
  193.8 8.0 %fusion.27 = f32[64,128,128]{1,2,0:T(8,128)} fusion(f32[64,128,128]{2,1,0:T(8,128)} %bitcast.23, f32[16,128,128]{2,1,0:T(8,128)S(1)} %multiply_add_fusion.1), kind=kOutput, calls=%fused_computation.87 | convolution fusion | flops 1610612736 | bytes 8454144 | tf_op jit(solution)/shard_map/nij,jk->nik/dot_general | solution.py:32
  201.8 8.1 %fusion.29 = f32[64,128,128]{1,2,0:T(8,128)} fusion(f32[64,128,128]{2,1,0:T(8,128)} %bitcast.23, f32[16,128,128]{2,1,0:T(8,128)S(1)} %multiply_add_fusion.1), kind=kOutput, calls=%fused_computation.91 | convolution fusion | flops 1610612736 | bytes 8454144 | tf_op jit(solution)/shard_map/nij,jk->nik/dot_general | solution.py:32
  210.0 6.0 %fusion.31 = f32[64,128,128]{1,2,0:T(8,128)S(1)} fusion(f32[64,128,128]{2,1,0:T(8,128)} %bitcast.23, f32[16,128,128]{2,1,0:T(8,128)S(1)} %multiply_add_fusion.1), kind=kOutput, calls=%fused_computation.95 | convolution fusion | flops 1610612736 | bytes 8454144 | tf_op jit(solution)/shard_map/nij,jk->nik/dot_general | solution.py:32
  216.0 5.6 %fusion.33 = f32[64,128,128]{1,2,0:T(8,128)S(1)} fusion(f32[64,128,128]{2,1,0:T(8,128)} %bitcast.23, f32[16,128,128]{2,1,0:T(8,128)S(1)} %multiply_add_fusion.1), kind=kOutput, calls=%fused_computation.99 | convolution fusion | flops 1610612736 | bytes 8454144 | tf_op jit(solution)/shard_map/nij,jk->nik/dot_general | solution.py:32
  221.6 5.6 %fusion.35 = f32[64,128,128]{1,2,0:T(8,128)S(1)} fusion(f32[64,128,128]{2,1,0:T(8,128)} %bitcast.23, f32[16,128,128]{2,1,0:T(8,128)S(1)} %multiply_add_fusion.1), kind=kOutput, calls=%fused_computation.103 | convolution fusion | flops 1610612736 | bytes 8454144 | tf_op jit(solution)/shard_map/nij,jk->nik/dot_general | solution.py:32
  227.2 5.6 %fusion.37 = f32[64,128,128]{1,2,0:T(8,128)S(1)} fusion(f32[64,128,128]{2,1,0:T(8,128)} %bitcast.23, f32[16,128,128]{2,1,0:T(8,128)S(1)} %multiply_add_fusion.1), kind=kOutput, calls=%fused_computation.107 | convolution fusion | flops 1610612736 | bytes 8454144 | tf_op jit(solution)/shard_map/nij,jk->nik/dot_general | solution.py:32
  232.9 5.6 %fusion.39 = f32[64,128,128]{1,2,0:T(8,128)S(1)} fusion(f32[64,128,128]{2,1,0:T(8,128)} %bitcast.23, f32[16,128,128]{2,1,0:T(8,128)S(1)} %multiply_add_fusion.1), kind=kOutput, calls=%fused_computation.111 | convolution fusion | flops 1610612736 | bytes 8454144 | tf_op jit(solution)/shard_map/nij,jk->nik/dot_general | solution.py:32
  238.5 5.8 %fusion.41 = f32[64,128,128]{1,2,0:T(8,128)S(1)} fusion(f32[64,128,128]{2,1,0:T(8,128)} %bitcast.23, f32[16,128,128]{2,1,0:T(8,128)S(1)} %multiply_add_fusion.1), kind=kOutput, calls=%fused_computation.115 | convolution fusion | flops 1610612736 | bytes 8454144 | tf_op jit(solution)/shard_map/nij,jk->nik/dot_general | solution.py:32
  244.3 5.6 %fusion.43 = f32[64,128,128]{1,2,0:T(8,128)S(1)} fusion(f32[64,128,128]{2,1,0:T(8,128)} %bitcast.23, f32[16,128,128]{2,1,0:T(8,128)S(1)} %multiply_add_fusion.1), kind=kOutput, calls=%fused_computation.119 | convolution fusion | flops 1610612736 | bytes 8454144 | tf_op jit(solution)/shard_map/nij,jk->nik/dot_general | solution.py:32
  249.9 5.6 %fusion.45 = f32[64,128,128]{1,2,0:T(8,128)S(1)} fusion(f32[64,128,128]{2,1,0:T(8,128)} %bitcast.23, f32[16,128,128]{2,1,0:T(8,128)S(1)} %multiply_add_fusion.1), kind=kOutput, calls=%fused_computation.123 | convolution fusion | flops 1610612736 | bytes 8454144 | tf_op jit(solution)/shard_map/nij,jk->nik/dot_general | solution.py:32
  255.5 5.8 %fusion.47 = f32[64,128,128]{1,2,0:T(8,128)S(1)} fusion(f32[64,128,128]{2,1,0:T(8,128)} %bitcast.23, f32[16,128,128]{2,1,0:T(8,128)S(1)} %multiply_add_fusion.1), kind=kOutput, calls=%fused_computation.127 | convolution fusion | flops 1610612736 | bytes 8454144 | tf_op jit(solution)/shard_map/nij,jk->nik/dot_general | solution.py:32
  261.4 8.1 %fusion.17 = f32[64,128,128]{1,2,0:T(8,128)} fusion(f32[64,128,128]{2,1,0:T(8,128)} %bitcast.23, f32[16,128,128]{2,1,0:T(8,128)S(1)} %multiply_add_fusion.1), kind=kOutput, calls=%fused_computation.67 | convolution fusion | flops 1610612736 | bytes 8454144 | tf_op jit(solution)/shard_map/nij,jk->nik/dot_general | solution.py:32
  269.4 6.6 %fusion.18 = f32[64,128,128]{2,1,0:T(8,128)} fusion(f32[64,128,128]{1,2,0:T(8,128)} %fusion.19, f32[16,128,128]{2,1,0:T(8,128)S(1)} %multiply_add_fusion), kind=kOutput, calls=%fused_computation.69 | convolution fusion | flops 1610612736 | bytes 8454144 | tf_op jit(solution)/shard_map/ij,njk->nik/dot_general | solution.py:39
  276.0 6.5 %fusion.20 = f32[64,128,128]{2,1,0:T(8,128)} fusion(f32[64,128,128]{1,2,0:T(8,128)} %fusion.21, f32[16,128,128]{2,1,0:T(8,128)S(1)} %multiply_add_fusion), kind=kOutput, calls=%fused_computation.73 | convolution fusion | flops 1610612736 | bytes 8454144 | tf_op jit(solution)/shard_map/ij,njk->nik/dot_general | solution.py:39
  282.5 6.6 %fusion.22 = f32[64,128,128]{2,1,0:T(8,128)} fusion(f32[64,128,128]{1,2,0:T(8,128)} %fusion.23, f32[16,128,128]{2,1,0:T(8,128)S(1)} %multiply_add_fusion), kind=kOutput, calls=%fused_computation.77 | convolution fusion | flops 1610612736 | bytes 8454144 | tf_op jit(solution)/shard_map/ij,njk->nik/dot_general | solution.py:39
  289.1 6.5 %fusion.24 = f32[64,128,128]{2,1,0:T(8,128)} fusion(f32[64,128,128]{1,2,0:T(8,128)} %fusion.25, f32[16,128,128]{2,1,0:T(8,128)S(1)} %multiply_add_fusion), kind=kOutput, calls=%fused_computation.81 | convolution fusion | flops 1610612736 | bytes 8454144 | tf_op jit(solution)/shard_map/ij,njk->nik/dot_general | solution.py:39
  295.7 7.0 %fusion.26 = f32[64,128,128]{2,1,0:T(8,128)} fusion(f32[64,128,128]{1,2,0:T(8,128)} %fusion.27, f32[16,128,128]{2,1,0:T(8,128)S(1)} %multiply_add_fusion), kind=kOutput, calls=%fused_computation.85 | convolution fusion | flops 1610612736 | bytes 8454144 | tf_op jit(solution)/shard_map/ij,njk->nik/dot_general | solution.py:39
  302.6 6.5 %fusion.28 = f32[64,128,128]{2,1,0:T(8,128)} fusion(f32[64,128,128]{1,2,0:T(8,128)} %fusion.29, f32[16,128,128]{2,1,0:T(8,128)S(1)} %multiply_add_fusion), kind=kOutput, calls=%fused_computation.89 | convolution fusion | flops 1610612736 | bytes 8454144 | tf_op jit(solution)/shard_map/ij,njk->nik/dot_general | solution.py:39
  354.5 70.8 %fusion.2 = f32[64,128,128,1]{1,2,0,3:T(8,128)} fusion(f32[64,128,128]{2,1,0:T(8,128)} %fusion.18, f32[64,128,128]{2,1,0:T(8,128)} %fusion.20, f32[64,128,128]{2,1,0:T(8,128)} %fusion.22, f32[64,128,128]{2,1,0:T(8,128)} %fusion.24, f32[64,128,128]{2,1,0:T(8,128)} %fusion.26, f32[64,128,128]{2,1,0:T(8,128)} %fusion.28, f32[64,128,128]{2,1,0:T(8,128)} %fusion.30, ...), kind=kOutput, calls=%fused_computation.8 | convolution fusion | flops 1729101824 | bytes 78217728 | tf_op jit(solution)/shard_map/ij,njk->nik/dot_general | solution.py:39
  441.0 7.4 %copy.194 = f32[32,2,128,128]{3,1,0,2:T(2,128)} copy(f32[32,2,128,128]{2,3,1,0:T(8,128)} %broadcast_divide_fusion) | data formatting | bytes 8388608 | tf_op jit(solution)/shard_map/div | solution.py:117
  458.5 23.4 %reduce-scatter.5.cloned.1.call-done = f32[64,256]{1,0:T(8,128)} async-done(((f32[256,256]{1,0:T(8,128)}), f32[64,256]{1,0:T(8,128)}) %reduce-scatter.5.cloned.1.call-update) | async-done | bytes 65552 | tf_op jit(solution)/shard_map/reduce_scatter | solution.py:142
  (316 shorter events, 141.8 us)
Async XLA Ops:
  7.2 48.4 %copy-start = (f32[1,1,32,128,128]{4,3,2,1,0:T(8,128)S(1)}, f32[1,1,32,128,128]{4,3,2,1,0:T(8,128)}, u32[]{:S(2)}) copy-start(f32[1,1,32,128,128]{4,3,2,1,0:T(8,128)} %param.12) | copy-start | bytes 6291460
  7.2 39.0 %copy-start.2 = (f32[16,41]{1,0:T(8,128)S(1)}, f32[16,41]{1,0:T(8,128)}, u32[]{:S(2)}) copy-start(f32[16,41]{1,0:T(8,128)} %param.19) | copy-start | bytes 7876
  13.7 66.8 %all-to-all-start = ((f32[32,2,4]{2,1,0:T(2,128)}), f32[32,2,4]{2,1,0:T(2,128)S(1)}, u32[]{:S(2)}, u32[]{:S(2)}) async-start(f32[32,2,4]{2,1,0:T(2,128)} %select_multiply_fusion.2), calls=%async_computation | async-start | bytes 65536 | tf_op jit(solution)/shard_map/all_to_all | solution.py:105
  58.4 6.8 %copy-start.93 = (s32[64]{0:T(128)S(1)}, s32[64]{0:T(128)}, u32[]{:S(2)}) copy-start(s32[64]{0:T(128)} %fusion.253) | copy-start | bytes 772
  67.9 6.7 %copy-start.20 = (f32[128,128]{1,0:T(8,128)S(1)}, f32[128,128]{1,0:T(8,128)}, u32[]{:S(2)}) copy-start(f32[128,128]{1,0:T(8,128)} %get-tuple-element.315) | copy-start | bytes 196612
  68.0 6.7 %copy-start.21 = (f32[128,128]{1,0:T(8,128)S(1)}, f32[128,128]{1,0:T(8,128)}, u32[]{:S(2)}) copy-start(f32[128,128]{1,0:T(8,128)} %get-tuple-element.312) | copy-start | bytes 196612
  68.0 6.7 %copy-start.22 = (f32[128,128]{1,0:T(8,128)S(1)}, f32[128,128]{1,0:T(8,128)}, u32[]{:S(2)}) copy-start(f32[128,128]{1,0:T(8,128)} %get-tuple-element.313) | copy-start | bytes 196612
  68.0 6.7 %copy-start.23 = (f32[128,128]{1,0:T(8,128)S(1)}, f32[128,128]{1,0:T(8,128)}, u32[]{:S(2)}) copy-start(f32[128,128]{1,0:T(8,128)} %get-tuple-element.310) | copy-start | bytes 196612
  68.0 6.7 %copy-start.24 = (f32[128,128]{1,0:T(8,128)S(1)}, f32[128,128]{1,0:T(8,128)}, u32[]{:S(2)}) copy-start(f32[128,128]{1,0:T(8,128)} %get-tuple-element.311) | copy-start | bytes 196612
  68.0 6.7 %copy-start.25 = (f32[128,128]{1,0:T(8,128)S(1)}, f32[128,128]{1,0:T(8,128)}, u32[]{:S(2)}) copy-start(f32[128,128]{1,0:T(8,128)} %get-tuple-element.308) | copy-start | bytes 196612
  68.0 6.7 %copy-start.26 = (f32[128,128]{1,0:T(8,128)S(1)}, f32[128,128]{1,0:T(8,128)}, u32[]{:S(2)}) copy-start(f32[128,128]{1,0:T(8,128)} %get-tuple-element.309) | copy-start | bytes 196612
  68.0 6.7 %copy-start.27 = (f32[128,128]{1,0:T(8,128)S(1)}, f32[128,128]{1,0:T(8,128)}, u32[]{:S(2)}) copy-start(f32[128,128]{1,0:T(8,128)} %get-tuple-element.306) | copy-start | bytes 196612
  68.0 6.7 %copy-start.28 = (f32[128,128]{1,0:T(8,128)S(1)}, f32[128,128]{1,0:T(8,128)}, u32[]{:S(2)}) copy-start(f32[128,128]{1,0:T(8,128)} %get-tuple-element.307) | copy-start | bytes 196612
  68.0 6.7 %copy-start.29 = (f32[128,128]{1,0:T(8,128)S(1)}, f32[128,128]{1,0:T(8,128)}, u32[]{:S(2)}) copy-start(f32[128,128]{1,0:T(8,128)} %get-tuple-element.304) | copy-start | bytes 196612
  68.0 6.7 %copy-start.30 = (f32[128,128]{1,0:T(8,128)S(1)}, f32[128,128]{1,0:T(8,128)}, u32[]{:S(2)}) copy-start(f32[128,128]{1,0:T(8,128)} %get-tuple-element.305) | copy-start | bytes 196612
  68.1 6.7 %copy-start.31 = (f32[128,128]{1,0:T(8,128)S(1)}, f32[128,128]{1,0:T(8,128)}, u32[]{:S(2)}) copy-start(f32[128,128]{1,0:T(8,128)} %get-tuple-element.302) | copy-start | bytes 196612
  68.1 6.7 %copy-start.32 = (f32[128,128]{1,0:T(8,128)S(1)}, f32[128,128]{1,0:T(8,128)}, u32[]{:S(2)}) copy-start(f32[128,128]{1,0:T(8,128)} %get-tuple-element.303) | copy-start | bytes 196612
  68.1 6.7 %copy-start.33 = (f32[128,128]{1,0:T(8,128)S(1)}, f32[128,128]{1,0:T(8,128)}, u32[]{:S(2)}) copy-start(f32[128,128]{1,0:T(8,128)} %get-tuple-element.300) | copy-start | bytes 196612
  68.1 6.7 %copy-start.34 = (f32[128,128]{1,0:T(8,128)S(1)}, f32[128,128]{1,0:T(8,128)}, u32[]{:S(2)}) copy-start(f32[128,128]{1,0:T(8,128)} %get-tuple-element.301) | copy-start | bytes 196612
  68.1 6.7 %copy-start.35 = (f32[128,128]{1,0:T(8,128)S(1)}, f32[128,128]{1,0:T(8,128)}, u32[]{:S(2)}) copy-start(f32[128,128]{1,0:T(8,128)} %get-tuple-element.298) | copy-start | bytes 196612
  68.1 6.7 %copy-start.36 = (f32[128,128]{1,0:T(8,128)S(1)}, f32[128,128]{1,0:T(8,128)}, u32[]{:S(2)}) copy-start(f32[128,128]{1,0:T(8,128)} %get-tuple-element.299) | copy-start | bytes 196612
  68.1 6.7 %copy-start.37 = (f32[128,128]{1,0:T(8,128)S(1)}, f32[128,128]{1,0:T(8,128)}, u32[]{:S(2)}) copy-start(f32[128,128]{1,0:T(8,128)} %get-tuple-element.296) | copy-start | bytes 196612
  68.1 6.7 %copy-start.38 = (f32[128,128]{1,0:T(8,128)S(1)}, f32[128,128]{1,0:T(8,128)}, u32[]{:S(2)}) copy-start(f32[128,128]{1,0:T(8,128)} %get-tuple-element.297) | copy-start | bytes 196612
  68.1 6.7 %copy-start.39 = (f32[128,128]{1,0:T(8,128)S(1)}, f32[128,128]{1,0:T(8,128)}, u32[]{:S(2)}) copy-start(f32[128,128]{1,0:T(8,128)} %get-tuple-element.294) | copy-start | bytes 196612
  68.1 6.7 %copy-start.40 = (f32[128,128]{1,0:T(8,128)S(1)}, f32[128,128]{1,0:T(8,128)}, u32[]{:S(2)}) copy-start(f32[128,128]{1,0:T(8,128)} %get-tuple-element.295) | copy-start | bytes 196612
  68.2 6.7 %copy-start.41 = (f32[128,128]{1,0:T(8,128)S(1)}, f32[128,128]{1,0:T(8,128)}, u32[]{:S(2)}) copy-start(f32[128,128]{1,0:T(8,128)} %get-tuple-element.292) | copy-start | bytes 196612
  80.5 14.8 %all-to-all-start.2 = ((f32[32,1,192]{2,1,0:T(1,128)}), f32[32,1,192]{2,1,0:T(1,128)S(1)}, u32[]{:S(2)}, u32[]{:S(2)}) async-start(f32[32,1,192]{2,1,0:T(1,128)} %reshape.5191), calls=%async_computation.2 | async-start | bytes 65536 | tf_op jit(solution)/shard_map/all_to_all | solution.py:102
  95.4 59.1 %all-to-all-start.3 = ((f32[32,2,128,128]{3,2,1,0:T(8,128)}), f32[32,2,128,128]{3,2,1,0:T(8,128)}, u32[]{:S(2)}, u32[]{:S(2)}) async-start(f32[32,2,128,128]{3,2,1,0:T(8,128)} %bitcast.539), calls=%async_computation.3 | async-start | bytes 8388608 | tf_op jit(solution)/shard_map/all_to_all | solution.py:100
  154.5 199.7 %all-to-all-start.1 = ((f32[32,2,128,128]{2,3,1,0:T(8,128)}), f32[32,2,128,128]{2,3,1,0:T(8,128)}, u32[]{:S(2)}, u32[]{:S(2)}) async-start(f32[32,2,128,128]{2,3,1,0:T(8,128)} %copy.170), calls=%async_computation.1 | async-start | bytes 8388608 | tf_op jit(solution)/shard_map/all_to_all | solution.py:101
  161.1 297.4 %reduce-scatter.3.cloned.1.call-start = ((), (), s32[]{:S(2)}) async-start(), calls=%async_computation.6 | async-start | bytes 327680 | tf_op jit(solution)/shard_map/reduce_scatter | solution.py:141
  436.2 45.7 %reduce-scatter.5.cloned.1.call-start = ((), (), s32[]{:S(2)}) async-start(), calls=%async_computation.7 | async-start | bytes 327680 | tf_op jit(solution)/shard_map/reduce_scatter | solution.py:142
  441.0 40.9 %copy-start.1 = (f32[1,1,32,128,128]{4,3,2,1,0:T(8,128)S(1)}, f32[1,1,32,128,128]{4,3,2,1,0:T(8,128)}, u32[]{:S(2)}) copy-start(f32[1,1,32,128,128]{4,3,2,1,0:T(8,128)} %param.12) | copy-start | bytes 6291460
  (68 other events, 398.9 us)
Sparse Core Ops, SparseCore 0:
  436.4 22.0 reduce-scatter.2
  461.6 20.2 reduce-scatter.4
where the time goes:
time: 498 us; the launch traced here: 489 us
  matrix products  272 us (55%)
  waiting for transfers between devices  70.5 us (14%)
  other arithmetic  51.2 us (10%)
  local copies, waits for them, and re-layouts  49.4 us (10%)
  starting transfers between devices  28.8 us (6%)
  between operations  16.9 us (3%)
    dot_general x16, matrix products, match_blocks(): jnp.einsum('ij,njk->nik', col_band[basis_index], spread, precision=highes...  155 us
    dot_general x16, matrix products, match_blocks(): jnp.einsum('nij,jk->nik', pixels, row_band[basis_index], precision=highes...  108 us
    all_to_all x1, waiting for transfers between devices, on_device(): lax.all_to_all(slot_pixels, 'patch', split_axis=0, concat_axis=0, tiled=T...  40.5 us
    reduce_scatter x1, waiting for transfers between devices, on_device(): lax.psum_scatter(weight_patch, 'visit', scatter_dimension=0, tiled=True)  23.4 us
    convert_element_type x42, other arithmetic, band_matrices(): picked = (offset == tap_index - radius).astype(jnp.float32)  22.7 us
    slice x6, local copies, waits for them, and re-layouts, band_matrices(): banded = banded + filter_taps[:, tap_index, None, None] * picked[None, :, :]  10.6 us
  transfers between devices with their start and end apart: 6, of which 4 were waited for; matrix products, arithmetic and copies ran while one was open for 58% of the time, Pallas kernels for 0%

commit v1 on v0

v1 whole, which is shorter than its diff:
```python
import functools

import jax
import jax.numpy as jnp
from jax import lax
from jax.experimental import pallas as pl
from jax.experimental.pallas import tpu as pltpu
from jax.sharding import PartitionSpec as P

highest = lax.Precision.HIGHEST
BLOCK = 128
TAPS = 41
NB = 16
TILE = 32
WIN = 80
LEAD = 24
GROUP = 8


def split(x):
    high = x.astype(jnp.bfloat16)
    return high, (x - high.astype(jnp.float32)).astype(jnp.bfloat16)


def split_outside(x):
    high = lax.reduce_precision(x, exponent_bits=8, mantissa_bits=7)
    return high.astype(jnp.bfloat16), (x - high).astype(jnp.bfloat16)


def toeplitz(taps, rows, columns, tap_of):
    at = tap_of(jnp.arange(rows)[:, None], jnp.arange(columns)[None, :])
    banded = jnp.zeros((taps.shape[0], rows, columns), jnp.float32)
    for tap in range(TAPS):
        banded = banded + taps[:, tap, None, None] * (at == tap).astype(jnp.float32)[None]
    return banded


def bands(row_taps, col_taps):
    col = toeplitz(col_taps, TILE, WIN, lambda r, s: r - s + LEAD + TAPS // 2)
    high, low = split_outside(col)
    left = jnp.concatenate([high, low, high, jnp.zeros((NB, TILE, 256 - 3 * WIN), jnp.bfloat16)], axis=2)
    left = left.reshape(NB * TILE, 256)
    row = toeplitz(row_taps, BLOCK, BLOCK, lambda i, j: j - i + TAPS // 2)
    high, low = split_outside(row)
    top = jnp.concatenate([high, low], axis=2)
    bottom = jnp.concatenate([high, jnp.zeros_like(low)], axis=2)
    return left, jnp.concatenate([top, bottom], axis=1)


def polynomials(table_rows, quadrants, coef_table):
    a = jnp.take(coef_table, table_rows, axis=0)
    down = (quadrants // 2).astype(jnp.float32)[:, None, None]
    across = (quadrants % 2).astype(jnp.float32)[:, None]
    u = (jnp.arange(BLOCK).astype(jnp.float32)[None, :] + 0.5) / BLOCK - 1.0 + across
    u = u[:, None, :]
    q = a[:, :, 0, None] + u * (a[:, :, 1, None] + u * a[:, :, 3, None])
    s = a[:, :, 2, None] + u * a[:, :, 4, None]
    e = jnp.broadcast_to(a[:, :, 5, None], q.shape)
    poly = jnp.stack([q + down * (s + down * e), s + 2.0 * down * e, e], axis=2)
    return poly.transpose(1, 2, 0, 3)[:, :, :, None, :]


def window(image_ref, block, tile):
    start = TILE * tile - LEAD
    low, high = max(start, 0), min(start + WIN, BLOCK)
    part = image_ref[block, low:high, :]
    pieces = []
    if low > start:
        pieces.append(jnp.zeros((low - start, BLOCK), jnp.float32))
    pieces.append(part)
    if high < start + WIN:
        pieces.append(jnp.zeros((start + WIN - high, BLOCK), jnp.float32))
    return jnp.concatenate(pieces, axis=0) if len(pieces) > 1 else part


def matched_tile(tile, group, image_ref, left_ref, right_ref, poly_ref, parts_ref, emit):
    first = group * GROUP
    for pair in range(GROUP // 2):
        both = jnp.concatenate(
            [window(image_ref, first + 2 * pair, tile), window(image_ref, first + 2 * pair + 1, tile)], axis=1
        )
        high, low = split(both)
        rhs = jnp.concatenate([high, high, low, jnp.zeros((256 - 3 * WIN, 2 * BLOCK), jnp.bfloat16)], axis=0)
        spread = jnp.dot(left_ref[...], rhs, preferred_element_type=jnp.float32)
        for side in range(2):
            high, low = split(spread[:, side * BLOCK : (side + 1) * BLOCK])
            at = (2 * pair + side) * TILE
            parts_ref[:, at : at + TILE, :BLOCK] = high.reshape(NB, TILE, BLOCK)
            parts_ref[:, at : at + TILE, BLOCK:] = low.reshape(NB, TILE, BLOCK)
    t = (lax.broadcasted_iota(jnp.int32, (TILE, BLOCK), 0).astype(jnp.float32) + (TILE * tile + 0.5)) / BLOCK - 1.0
    total = [None] * GROUP
    for k in range(NB):
        both = jnp.dot(parts_ref[k], right_ref[k], preferred_element_type=jnp.float32)
        basis = both[:, :BLOCK] + both[:, BLOCK:]
        for block in range(GROUP):
            q = poly_ref[k, 0, first + block]
            s = poly_ref[k, 1, first + block]
            e = poly_ref[k, 2, first + block]
            term = (q + t * (s + t * e)) * basis[block * TILE : (block + 1) * TILE]
            total[block] = term if total[block] is None else total[block] + term
    for block in range(GROUP):
        emit(first + block, total[block])


def local_kernel(live_ref, image_ref, variance_ref, left_ref, right_ref, poly_ref, weighted_ref, inverse_ref, parts_ref):
    live = live_ref[0]

    def step(group, carry):
        for block in range(GROUP):
            at = group * GROUP + block
            flag = (at < live).astype(jnp.float32)
            inverse_ref[at] = flag / variance_ref[at]
        for tile in range(BLOCK // TILE):

            def emit(at, total, tile=tile):
                rows = slice(tile * TILE, (tile + 1) * TILE)
                weighted_ref[at, rows, :] = inverse_ref[at, rows, :] * total

            matched_tile(tile, group, image_ref, left_ref, right_ref, poly_ref, parts_ref, emit)
        return carry

    lax.fori_loop(0, image_ref.shape[0] // GROUP, step, 0)


def local_blocks(live, pixels, variances, left, right, poly):
    vmem = pl.BlockSpec(memory_space=pltpu.VMEM)
    return pl.pallas_call(
        local_kernel,
        out_shape=(jax.ShapeDtypeStruct(pixels.shape, jnp.float32),) * 2,
        in_specs=[pl.BlockSpec(memory_space=pltpu.SMEM)] + [vmem] * 5,
        out_specs=(vmem, vmem),
        scratch_shapes=[pltpu.VMEM((NB, GROUP * TILE, 2 * BLOCK), jnp.bfloat16)],
        compiler_params=pltpu.CompilerParams(vmem_limit_bytes=48 << 20),
        name="match_blocks",
    )(live, pixels, variances, left, right, poly)


def on_device(
    image, variance, dest_patch, quadrant, coef_index, block_count, coef_table, row_taps, col_taps
):
    pixels = image[0, 0]
    variances = variance[0, 0]
    targets = dest_patch[0, 0]
    quadrants = quadrant[0, 0]
    table_rows = coef_index[0, 0]
    live_count = block_count[0, 0]
    blocks = pixels.shape[0]
    block_side = pixels.shape[-1]
    left, right = bands(row_taps, col_taps)
    poly = polynomials(table_rows, quadrants, coef_table)
    weighted, inverse = local_blocks(block_count[0], pixels, variances, left, right, poly)
    owners = lax.axis_size("patch")
    capacity = 2
    slot_total = owners * capacity
    position = jnp.arange(blocks)
    is_live = position < live_count
    earlier_same = (targets[:, None] == targets[None, :]) & is_live[None, :] & (position[None, :] < position[:, None])
    slot_rank = jnp.sum(earlier_same.astype(jnp.int32), axis=1)
    slot_of = jnp.where(is_live, targets * capacity + slot_rank, -1)
    slot_match = slot_of[None, :] == jnp.arange(slot_total)[:, None]
    occupied = jnp.any(slot_match, axis=1)
    source = jnp.sum(slot_match.astype(jnp.int32) * position[None, :], axis=1)
    presence = occupied.astype(jnp.float32)
    quarter_hot = (quadrants[:, None] == jnp.arange(4)[None, :]).astype(jnp.float32)
    slot_quarter = (jnp.take(quarter_hot, source, axis=0) * presence[:, None]).reshape(owners, capacity, 4)
    grid_shape = (owners, capacity, block_side, block_side)
    slot_weighted = (jnp.take(weighted, source, axis=0) * presence[:, None, None]).reshape(grid_shape)
    slot_inverse = (jnp.take(inverse, source, axis=0) * presence[:, None, None]).reshape(grid_shape)
    send = functools.partial(lax.all_to_all, axis_name="patch", split_axis=0, concat_axis=0, tiled=True)
    got_quarter = send(slot_quarter).reshape(-1, 2, 2)
    patches = []
    for got in (send(slot_weighted), send(slot_inverse)):
        patch = jnp.einsum(
            "nab,nij->aibj", got_quarter, got.reshape(-1, block_side, block_side),
            precision=highest, preferred_element_type=jnp.float32,
        ).reshape(2 * block_side, 2 * block_side)
        patches.append(lax.psum_scatter(patch, "visit", scatter_dimension=0, tiled=True)[None])
    return tuple(patches)


def solution(mesh):
    placed = (
        P("visit", "patch", None, None, None),
        P("visit", "patch", None, None, None),
        P("visit", "patch", None),
        P("visit", "patch", None),
        P("visit", "patch", None),
        P("visit", "patch"),
        P(),
        P(),
        P(),
    )
    return jax.shard_map(
        on_device,
        mesh=mesh,
        in_specs=placed,
        out_specs=(P("patch", "visit", None), P("patch", "visit", None)),
        check_vma=False,
    )
```

time: 498 us -> 250 us (0.50)
  the two profiles are of different devices: /device:TPU:0 before, /device:TPU:1 now
where the time goes in v1:
time: 250 us; the launch traced here: 248 us
  waiting for transfers between devices  61.8 us (25%)
  blocking collectives  58.1 us (23%)
  local copies, waits for them, and re-layouts  42.5 us (17%)
  other arithmetic  31 us (12%)
  Pallas kernels  20.3 us (8%)
  between operations  15.3 us (6%)
  starting transfers between devices  14.4 us (6%)
  matrix products  4.53 us (2%)
    all_to_all x1, blocking collectives, on_device(): send(slot_inverse)  58.1 us
    all_to_all x1, waiting for transfers between devices, on_device(): send(slot_weighted)  42.4 us
    pallas_call x1, Pallas kernels, local_blocks(): pl.pallas_call(local_kernel, out_shape=(jax.ShapeDtypeStruct(pixels.shape...  20.3 us
    reduce_scatter x2, waiting for transfers between devices, on_device(): lax.psum_scatter(patch, 'visit', scatter_dimension=0, tiled=True)[None]  19.4 us
    slice x6, local copies, waits for them, and re-layouts, toeplitz(): taps[:, tap, None, None] * (at == tap).astype(jnp.float32)[None]  9.79 us
    all_to_all x1, starting transfers between devices, on_device(): got_quarter = send(slot_quarter).reshape(-1, 2, 2)  9.49 us
    mul x1, other arithmetic, on_device(): jnp.take(inverse, source, axis=0) * presence[:, None, None]  8.56 us
    convert_element_type x4, other arithmetic, split_outside(): return (high.astype(jnp.bfloat16), (x - high).astype(jnp.bfloat16))  8.42 us
  transfers between devices with their start and end apart: 4, of which 2 were waited for; matrix products, arithmetic and copies ran while one was open for 29% of the time, Pallas kernels for 8%

profile of v1, /device:TPU:1, one launch (start us, length us, event | category | flops | bytes accessed | tf_op | source)
XLA Modules:
  0.0 248.0 jit_solution(7444296969384738006)
XLA Ops:
  7.9 0.9 convert_reduce_fusion
  11.2 0.8 select_multiply_fusion.2
  12.0 9.5 %all-to-all-start.1 = ((f32[32,2,4]{2,1,0:T(2,128)}), f32[32,2,4]{2,1,0:T(2,128)}, u32[]{:S(2)}, u32[]{:S(2)}) async-start(f32[32,2,4]{2,1,0:T(2,128)} %select_multiply_fusion.2), calls=%async_computation.1 | async-start | bytes 65536 | tf_op jit(solution)/shard_map/all_to_all | solution.py:170
  21.4 1.9 slice_reduce_fusion.40
  23.4 1.9 slice_reduce_fusion.39
  25.3 1.0 slice_reduce_fusion.38
  26.9 1.9 slice_reduce_fusion.81
  28.8 1.9 slice_reduce_fusion.80
  30.8 1.0 slice_reduce_fusion.79
  34.9 3.9 %fusion.2 = (bf16[16,128,128]{2,1,0:T(8,128)(2,1)}, f32[16,128,128]{2,1,0:T(8,128)S(1)}) fusion(f32[128,128]{1,0:T(8,128)S(1)} %fusion.125, f32[16]{0:T(128)S(1)} %get-tuple-element.46, f32[128,128]{1,0:T(8,128)S(1)} %get-tuple-element.184, f32[16]{0:T(128)S(1)} %get-tuple-element.47, f32[128,128]{1,0:T(8,128)S(1)} %get-tuple-element.183, ...), kind=kLoop, calls=%fused_computation.13 | loop fusion | flops 22020096 | bytes 4262464 | tf_op jit(solution)/shard_map/convert_element_type | solution.py:27
  38.8 0.9 reduce-precision_convert_fusion
  45.9 3.0 %fusion.3 = (bf16[512,80]{1,0:T(8,128)(2,1)S(1)}, f32[512,80]{1,0:T(8,128)S(1)}) fusion(f32[32,80]{1,0:T(8,128)S(1)} %fusion.208, f32[512]{0:T(512)S(1)} %mul.2033, f32[32,80]{1,0:T(8,128)S(1)} %get-tuple-element.144, f32[512]{0:T(512)S(1)} %mul.2026, f32[32,80]{1,0:T(8,128)S(1)} %get-tuple-element.143, f32[512]{0:T(512)S(1)} %mul.2019, ...), kind=kLoop, calls=%fused_computation.18 | loop fusion | flops 3440640 | bytes 749568 | tf_op jit(solution)/shard_map/convert_element_type | solution.py:27
  49.5 2.6 %copy.38 = f32[800,16,6]{1,2,0:T(8,128)S(1)} copy(f32[800,16,6]{0,1,2:T(8,128)} %param.17) | data formatting | bytes 614400 | tf_op args[6]
  52.7 0.8 broadcast_select_fusion
  54.6 3.0 %fusion.1.right_ref = bf16[16,256,256]{2,1,0:T(8,128)(2,1)} fusion(bf16[16,128,128]{2,1,0:T(8,128)(2,1)} %reduce-precision_convert_fusion, bf16[16,128,128]{2,1,0:T(8,128)(2,1)} %get-tuple-element.91), kind=kLoop, calls=%fused_computation.8 | loop fusion | flops 8388608 | bytes 3145728 | tf_op jit(solution)/shard_map/concatenate | solution.py:47
  57.7 0.7 broadcast_add_fusion
  58.4 1.2 maximum_maximum_fusion.left_ref
  59.6 1.1 multiply_add_fusion.2
  60.9 20.3 %match_blocks.1 = (f32[32,128,128]{2,1,0:T(8,128)S(1)}, f32[32,128,128]{2,1,0:T(8,128)S(1)}) custom-call(s32[1]{0:T(128)} %bitcast.354.live_ref, f32[32,128,128]{2,1,0:T(8,128)} %bitcast.360, f32[32,128,128]{2,1,0:T(8,128)} %bitcast.361, bf16[512,256]{1,0:T(8,128)(2,1)S(1)} %maximum_maximum_fusion.left_ref, bf16[16,256,256]{2,1,0:T(8,128)(2,1)} %fusion.1.right_ref, ...), custom_call_target="tpu_custom_call" | custom-call | tf_op jit(solution)/shard_map/match_blocks/pallas_call | solution.py:127
  81.2 1.3 copy-done
  82.5 4.4 %gather_fusion.2 = f32[64,128,128]{2,1,0:T(8,128)} fusion(f32[32,128,128]{2,1,0:T(8,128)} %copy-done, s32[1024]{0:T(1024)S(1)} %pad_clamp_fusion.1), kind=kCustom, calls=%fused_computation.clone | custom fusion | bytes 8388864 | tf_op jit(solution)/shard_map/jit(_take)/gather | solution.py:167
  86.9 2.7 %gather_fusion.3 = f32[64,128,128]{2,1,0:T(8,128)} fusion(f32[32,128,128]{2,1,0:T(8,128)S(1)} %get-tuple-element.6, s32[1024]{0:T(1024)S(1)} %pad_clamp_fusion.1), kind=kCustom, calls=%fused_computation.1.clone | custom fusion | bytes 8388864 | tf_op jit(solution)/shard_map/jit(_take)/gather | solution.py:168
  89.6 8.6 %select_multiply_fusion = (f32[64,128,128]{2,1,0:T(8,128)}, f32[64,128,128]{2,1,0:T(8,128)}) fusion(f32[64,128,128]{2,1,0:T(8,128)} %gather_fusion.3, f32[64]{0:T(128)S(1)} %convert_element_type.726, pred[64]{0:T(512)(128)(4,1)S(1)} %compare_and_fusion.1, f32[64,128,128]{2,1,0:T(8,128)} %gather_fusion.2), kind=kLoop, calls=%fused_computation.5 | loop fusion | flops 4194304 | bytes 16777536 | tf_op jit(solution)/shard_map/mul | solution.py:168
  98.2 58.1 %all_to_all.15 = f32[32,2,128,128]{3,2,1,0:T(8,128)} all-to-all(f32[32,2,128,128]{3,2,1,0:T(8,128)} %bitcast.359), channel_id=1, replica_groups=mesh['visit'=4,'patch'=32] {'patch'}, dimensions={0} | all-to-all | bytes 8388608 | tf_op jit(solution)/shard_map/all_to_all | solution.py:172
  156.3 4.7 %all-to-all-start = ((f32[32,2,128,128]{3,2,1,0:T(8,128)}), f32[32,2,128,128]{3,2,1,0:T(8,128)}, u32[]{:S(2)}, u32[]{:S(2)}) async-start(f32[32,2,128,128]{3,2,1,0:T(8,128)} %bitcast.358), calls=%async_computation | async-start | bytes 8388608 | tf_op jit(solution)/shard_map/all_to_all | solution.py:172
  161.2 0.9 reshape.1547
  162.2 5.4 %copy.48 = f32[32,2,128,128]{3,1,0,2:T(2,128)S(1)} copy(f32[32,2,128,128]{3,2,1,0:T(8,128)} %all_to_all.15) | data formatting | bytes 8388608 | tf_op jit(solution)/shard_map/all_to_all | solution.py:172
  167.6 2.3 convolution_bitcast_fusion
  170.8 42.4 %all-to-all-done = f32[32,2,128,128]{3,2,1,0:T(8,128)} async-done(((f32[32,2,128,128]{3,2,1,0:T(8,128)}), f32[32,2,128,128]{3,2,1,0:T(8,128)}, u32[]{:S(2)}, u32[]{:S(2)}) %all-to-all-start) | async-done | bytes 4194336 | tf_op jit(solution)/shard_map/all_to_all | solution.py:172
  213.1 5.4 %copy.45 = f32[32,2,128,128]{3,1,0,2:T(2,128)S(1)} copy(f32[32,2,128,128]{3,2,1,0:T(8,128)} %all-to-all-done) | data formatting | bytes 8388608 | tf_op jit(solution)/shard_map/all_to_all | solution.py:172
  218.6 2.3 convolution_bitcast_fusion.1
  221.7 19.4 %reduce-scatter.3.cloned.1.call-done = f32[64,256]{1,0:T(8,128)} async-done(((f32[256,256]{1,0:T(8,128)}), f32[64,256]{1,0:T(8,128)}) %reduce-scatter.3.cloned.1.call-update) | async-done | bytes 65552 | tf_op jit(solution)/shard_map/reduce_scatter | solution.py:177
  (174 shorter events, 16.6 us)
Async XLA Ops:
  7.2 25.6 %copy-start.1 = (s32[1,1,32]{2,1,0:T(1,128)S(1)}, s32[1,1,32]{2,1,0:T(1,128)}, u32[]{:S(2)}) copy-start(s32[1,1,32]{2,1,0:T(1,128)} %param.14) | copy-start | bytes 388
  7.2 24.9 %copy-start.2 = (s32[1,1,32]{2,1,0:T(1,128)S(1)}, s32[1,1,32]{2,1,0:T(1,128)}, u32[]{:S(2)}) copy-start(s32[1,1,32]{2,1,0:T(1,128)} %param.15) | copy-start | bytes 388
  12.0 86.2 %all-to-all-start.1 = ((f32[32,2,4]{2,1,0:T(2,128)}), f32[32,2,4]{2,1,0:T(2,128)}, u32[]{:S(2)}, u32[]{:S(2)}) async-start(f32[32,2,4]{2,1,0:T(2,128)} %select_multiply_fusion.2), calls=%async_computation.1 | async-start | bytes 65536 | tf_op jit(solution)/shard_map/all_to_all | solution.py:170
  81.1 1.4 copy-start
  156.3 56.9 %all-to-all-start = ((f32[32,2,128,128]{3,2,1,0:T(8,128)}), f32[32,2,128,128]{3,2,1,0:T(8,128)}, u32[]{:S(2)}, u32[]{:S(2)}) async-start(f32[32,2,128,128]{3,2,1,0:T(8,128)} %bitcast.358), calls=%async_computation | async-start | bytes 8388608 | tf_op jit(solution)/shard_map/all_to_all | solution.py:172
  160.9 60.7 %reduce-scatter.5.cloned.1.call-start = ((), (), s32[]{:S(2)}) async-start(), calls=%async_computation.6 | async-start | bytes 327680 | tf_op jit(solution)/shard_map/reduce_scatter | solution.py:177
  170.7 70.4 %reduce-scatter.3.cloned.1.call-start = ((), (), s32[]{:S(2)}) async-start(), calls=%async_computation.5 | async-start | bytes 327680 | tf_op jit(solution)/shard_map/reduce_scatter | solution.py:177
Sparse Core Ops, SparseCore 0:
  170.9 20.4 reduce-scatter.4
  221.8 19.2 reduce-scatter.2

commit v2 on v1

v2 whole, which is shorter than its diff:
```python
import functools
import itertools

import jax
import jax.numpy as jnp
from jax import lax
from jax.experimental import pallas as pl
from jax.experimental.pallas import tpu as pltpu
from jax.sharding import PartitionSpec as P

BLOCK = 128
TAPS = 41
REACH = TAPS // 2
NB = 16
BLOCKS = 32
TILE = 32
WIN = 80
LEAD = 24
GROUP = 8
STRIP = 8
SIDE = 4
SLOTS = 128
SLAB = BLOCKS * STRIP
MESH = pl.DeviceIdType.MESH
UNITS = ((0, 0, "x"), (0, 1, "z"), (1, 0, "y"), (1, 1, "y"))
AXES = ("x", "y", "z")


def split(x):
    high = x.astype(jnp.bfloat16)
    return high, (x - high.astype(jnp.float32)).astype(jnp.bfloat16)


def tap_rows(row_taps, col_taps):
    def parts(x):
        high = lax.reduce_precision(x, exponent_bits=8, mantissa_bits=7)
        return high, lax.reduce_precision(x - high, exponent_bits=8, mantissa_bits=7)

    def zeros(width):
        return jnp.zeros((NB, width), jnp.float32)

    high, low = parts(col_taps[:, ::-1])
    gap = zeros(WIN - TAPS)
    lead = LEAD - REACH
    row_high, row_low = parts(row_taps)
    around = zeros(BLOCK - TAPS)
    return jnp.concatenate(
        [
            zeros(lead), high, gap, low, gap, high, zeros(256 - 2 * WIN - lead - TAPS),
            row_high[:, REACH:], around, row_high[:, :REACH],
            row_low[:, REACH:], around, row_low[:, :REACH],
        ],
        axis=1,
    )


def build_bands(rows_ref, left_ref, right_ref):
    near = lax.broadcasted_iota(jnp.int32, (BLOCK, BLOCK), 1) - lax.broadcasted_iota(jnp.int32, (BLOCK, BLOCK), 0)
    near = (near <= REACH) & (near >= -REACH)

    def roll(row, height):
        return pltpu.roll(jnp.broadcast_to(row, (height, row.shape[1])), 0, 1, stride=1, stride_axis=0)

    for k in range(NB):
        band = roll(rows_ref[k : k + 1, :256], TILE)
        left_ref[k * TILE : (k + 1) * TILE, :] = band.astype(jnp.bfloat16)
        high = jnp.where(near, roll(rows_ref[k : k + 1, 256 : 256 + BLOCK], BLOCK), 0.0).astype(jnp.bfloat16)
        low = jnp.where(near, roll(rows_ref[k : k + 1, 256 + BLOCK :], BLOCK), 0.0).astype(jnp.bfloat16)
        right_ref[k, :BLOCK, :BLOCK] = high
        right_ref[k, :BLOCK, BLOCK:] = low
        right_ref[k, BLOCK:, :BLOCK] = high
        right_ref[k, BLOCK:, BLOCK:] = jnp.zeros_like(low)


def build_polynomials(coef_ref, quadrant_ref, poly_ref):
    column = lax.broadcasted_iota(jnp.int32, (NB, BLOCK), 1).astype(jnp.float32)
    own = (column + 0.5) / BLOCK - 1.0

    def build(b, carry):
        quadrant = quadrant_ref[b]
        down = (quadrant // 2).astype(jnp.float32)
        u = own + (quadrant % 2).astype(jnp.float32)
        a = coef_ref[b]
        a = [jnp.broadcast_to(a[:, m : m + 1], (NB, BLOCK)) for m in range(6)]
        q = a[0] + u * (a[1] + u * a[3])
        s = a[2] + u * a[4]
        e = a[5]
        poly_ref[b, 0] = q + down * (s + down * e)
        poly_ref[b, 1] = s + (2.0 * down) * e
        poly_ref[b, 2] = e
        return carry

    lax.fori_loop(0, BLOCKS, build, 0)


def window(image_ref, block, tile):
    start = TILE * tile - LEAD
    low, high = max(start, 0), min(start + WIN, BLOCK)
    part = image_ref[block, low:high, :]
    pieces = []
    if low > start:
        pieces.append(jnp.zeros((low - start, BLOCK), jnp.float32))
    pieces.append(part)
    if high < start + WIN:
        pieces.append(jnp.zeros((start + WIN - high, BLOCK), jnp.float32))
    return jnp.concatenate(pieces, axis=0) if len(pieces) > 1 else part


def matched_tile(tile, first, image_ref, left_ref, right_ref, poly_ref, parts_ref, emit):
    for pair in range(GROUP // 2):
        both = jnp.concatenate(
            [window(image_ref, first + 2 * pair, tile), window(image_ref, first + 2 * pair + 1, tile)], axis=1
        )
        high, low = split(both)
        rhs = jnp.concatenate([high, high, low, jnp.zeros((256 - 3 * WIN, 2 * BLOCK), jnp.bfloat16)], axis=0)
        spread = jnp.dot(left_ref[...], rhs, preferred_element_type=jnp.float32)
        for side in range(2):
            high, low = split(spread[:, side * BLOCK : (side + 1) * BLOCK])
            at = (2 * pair + side) * TILE
            parts_ref[:, at : at + TILE, :BLOCK] = high.reshape(NB, TILE, BLOCK)
            parts_ref[:, at : at + TILE, BLOCK:] = low.reshape(NB, TILE, BLOCK)
    t = (lax.broadcasted_iota(jnp.int32, (TILE, BLOCK), 0).astype(jnp.float32) + (TILE * tile + 0.5)) / BLOCK - 1.0
    total = [None] * GROUP
    for k in range(NB):
        both = jnp.dot(parts_ref[k], right_ref[k], preferred_element_type=jnp.float32)
        basis = both[:, :BLOCK] + both[:, BLOCK:]
        for block in range(GROUP):
            q = poly_ref[first + block, 0, k : k + 1, :]
            s = poly_ref[first + block, 1, k : k + 1, :]
            e = poly_ref[first + block, 2, k : k + 1, :]
            term = (q + t * (s + t * e)) * basis[block * TILE : (block + 1) * TILE]
            total[block] = term if total[block] is None else total[block] + term
    for block in range(GROUP):
        emit(first + block, total[block])


class Here:
    def __init__(self):
        self.y = lax.axis_index("visit")
        place = lax.axis_index("patch")
        self.x, self.z, self.c = lax.div(place, 8), lax.rem(lax.div(place, 2), 4), lax.rem(place, 2)
        self.odd = lax.rem(self.y + self.c, 2)

    def strip(self, axis):
        return getattr(self, axis) * 2 + self.c

    def at(self, c=0, **offsets):
        place = {axis: lax.rem(getattr(self, axis) + offsets.get(axis, 0), SIDE) for axis in AXES}
        place["c"] = lax.rem(self.c + c, 2)
        place["id"] = (place["y"], (place["x"] * SIDE + place["z"]) * 2 + place["c"])
        return place


def partners():
    found = set()
    for axis in AXES:
        others = [a for a in AXES if a != axis]
        for step, c in itertools.product(range(SIDE), range(2)):
            found.add(tuple(step if a == axis else 0 for a in AXES) + (c,))
        for steps in itertools.product(range(SIDE), repeat=2):
            to = dict(zip(others, steps))
            found.add(tuple(to.get(a, 0) for a in AXES) + (0,))
    found.discard((0, 0, 0, 0))
    return sorted(found)


def slot_rows(meta_ref, axis, here):
    patch, quadrant, live = meta_ref[0:1, :], meta_ref[1:2, :], meta_ref[2:3, :]
    x, z, c = lax.div(patch, 8), lax.rem(lax.div(patch, 2), 4), lax.rem(patch, 2)
    down, across = lax.div(quadrant, 2), lax.rem(quadrant, 2)
    if axis == "y":
        slot = (x * 4 + z) * 8 + c * 4 + down * 2 + across
    elif axis == "x":
        slot = (z * 2 + down) * 16 + (x * 2 + c) * 2 + across
    else:
        slot = (x * 2 + down) * 16 + (z * 2 + c) * 2 + across
    lane = lax.broadcasted_iota(jnp.int32, slot.shape, 1)
    mine = (lane >= here.strip(axis) * BLOCKS) & (lane < here.strip(axis) * BLOCKS + BLOCKS) & (live > 0)
    return jnp.broadcast_to(jnp.where(mine, slot, -1), (8, 256))


def fused_kernel(
    count_ref, quadrant_ref, image_ref, variance_ref, rows_ref, coef_ref, meta_ref, weighted_ref, weight_ref,
    left_ref, right_ref, poly_ref, parts_ref, strips_ref, slots_ref, got_slots_ref, got_ref, dense_ref, sums_y_ref, sums_ref,
    final_ref, got_final_ref,
    slots_send, slots_recv, first_send, first_recv, second_send, second_recv, third_send, third_recv,
):
    here = Here()
    barrier = pltpu.get_barrier_semaphore()
    all_partners = partners()
    for x, y, z, c in all_partners:
        pl.semaphore_signal(barrier, inc=1, device_id=here.at(x=x, y=y, z=z, c=c)["id"], device_id_type=MESH)

    live = count_ref[0]

    def invert(b, carry):
        flag = (b < live).astype(jnp.float32)
        rows = pl.ds(pl.multiple_of(b * STRIP, STRIP), STRIP)
        for chunk in range(BLOCK // STRIP):
            core, half, step = chunk // 8, chunk // 4 % 2, chunk % 4
            strips_ref[half * 8 + step * 2 + core, rows, :] = flag / variance_ref[b, chunk * STRIP : (chunk + 1) * STRIP, :]
        return carry

    lax.fori_loop(0, BLOCKS, invert, 0)
    for at, axis in enumerate(AXES):
        slots_ref[at] = slot_rows(meta_ref, axis, here)
    pl.semaphore_wait(barrier, len(all_partners))

    def remote(src, dst, send, recv, to):
        return pltpu.make_async_remote_copy(
            src_ref=src, dst_ref=dst, send_sem=send, recv_sem=recv, device_id=to["id"], device_id_type=MESH
        )

    def slots_copy(at, o):
        to = here.at(c=o % 2, **{AXES[at]: o // 2})
        return remote(slots_ref.at[at], got_slots_ref.at[at * 8 + o], slots_send.at[at, o], slots_recv.at[at, o], to)

    for at in range(3):
        for o in range(1, 8):
            slots_copy(at, o).start()

    def first_copy(unit, o, rows):
        axis = UNITS[unit][2]
        to = here.at(c=o % 2, **{axis: o // 2})
        source = strips_ref.at[unit * 8 + to[axis] * 2 + to["c"], rows, :]
        target = got_ref.at[unit * 8 + here.strip(axis), rows, :]
        if o == 0:
            return pltpu.make_async_copy(source, target, first_recv.at[unit, 0])
        return remote(source, target, first_send.at[unit, o], first_recv.at[unit, o], to)

    everything = pl.ds(0, SLAB)
    for unit in range(2):
        for o in range(8):
            first_copy(unit, o, everything).start()

    build_bands(rows_ref, left_ref, right_ref)
    build_polynomials(coef_ref, quadrant_ref, poly_ref)

    def compute(half):
        unit = 2 + half

        def step(group, carry):
            first = group * GROUP
            for core in range(2):

                def emit(b, total, core=core):
                    rows = pl.ds(pl.multiple_of(b * STRIP, STRIP), STRIP)
                    for step in range(SIDE):
                        at = step * 2 + core
                        strips_ref[unit * 8 + at, rows, :] = (
                            strips_ref[half * 8 + at, rows, :] * total[step * STRIP : (step + 1) * STRIP]
                        )

                matched_tile(core * 2 + half, first, image_ref, left_ref, right_ref, poly_ref, parts_ref, emit)
            rows = pl.ds(pl.multiple_of(group * GROUP * STRIP, GROUP * STRIP), GROUP * STRIP)
            for o in range(8):
                first_copy(unit, o, rows).start()
            return carry

        lax.fori_loop(0, BLOCKS // GROUP, step, 0)

    def take_slots(at):
        for o in range(1, 8):
            slots_copy(at, o).wait_recv()

    def second_copies(unit):
        axis = UNITS[unit][2]
        if axis == "y":
            for o in range(16):
                to = here.at(x=o // 4, z=o % 4)
                base = pl.multiple_of((to["x"] * SIDE + to["z"]) * 8, 8)
                yield o, to, dense_ref.at[unit, :, pl.ds(base, 8), :], sums_y_ref.at[unit - 2, o], o, o == 0
        else:
            other = "z" if axis == "x" else "x"
            for o in range(8):
                rise = here.odd + 2 * (o % 2)
                to = here.at(**{other: o // 2, "y": rise})
                base = pl.multiple_of((to[other] * 2 + lax.div(to["y"], 2)) * 16, 16)
                where = (o // 2) * 4 + rise
                yield o, to, dense_ref.at[unit, :, pl.ds(base, 16), :], sums_ref.at[unit, where], where, here.odd == 0 if o == 0 else False

    def start_second(unit):
        for o, to, source, target, where, own in second_copies(unit):
            away = remote(source, target, second_send.at[unit, o], second_recv.at[unit, where], to)
            home = pltpu.make_async_copy(source, target, second_recv.at[unit, where])
            if own is True:
                home.start()
            elif own is False:
                away.start()
            else:
                pl.when(own)(home.start)
                pl.when(jnp.logical_not(own))(away.start)

    def end_second(unit):
        for o, to, source, target, where, own in second_copies(unit):
            away = remote(source, target, second_send.at[unit, o], second_recv.at[unit, where], to)
            if own is True:
                continue
            if own is False:
                away.wait_send()
            else:
                pl.when(jnp.logical_not(own))(away.wait_send)

    def gather(unit):
        axis = UNITS[unit][2]
        for o in range(8):
            if o == 0:
                first_copy(unit, 0, everything).wait()
            else:
                first_copy(unit, o, everything).wait_recv()
        slots = slots_ref[AXES.index(axis)]
        for o in range(1, 8):
            slots = jnp.maximum(slots, got_slots_ref[AXES.index(axis) * 8 + o])
        hot = lax.broadcasted_iota(jnp.int32, (SLOTS, 256), 0) == slots[0:1, :]
        hot = hot.astype(jnp.float32).astype(jnp.bfloat16)
        for row in range(STRIP):
            data = jnp.concatenate(
                [got_ref[unit * 8 + o, pl.ds(row, BLOCKS, stride=STRIP), :] for o in range(8)], axis=0
            )
            both = jnp.dot(hot, jnp.concatenate(split(data), axis=1), preferred_element_type=jnp.float32)
            dense_ref[unit, row] = both[:, :BLOCK] + both[:, BLOCK:]
        start_second(unit)

    def third_copies(unit):
        axis = UNITS[unit][2]
        if axis == "y":
            for o in range(4):
                down, c = o // 2, o % 2
                to = here.at(c=c)
                owner = here.c + 2 * down
                to["id"] = (owner, to["id"][1])
                yield o, to, to["c"] * 2 + down, (owner == here.y if c == 0 else False)
        else:
            for o in range(8):
                to = here.at(c=o % 2, **{axis: o // 2})
                yield o, to, to[axis] * 2 + to["c"], o == 0

    def third_refs(unit, o, to, at):
        axis = UNITS[unit][2]
        source = final_ref.at[unit, pl.ds(pl.multiple_of(at * 16, 16), 16), :]
        where = getattr(here, axis)
        target = got_final_ref.at[unit, where]
        away = remote(source, target, third_send.at[unit, o], third_recv.at[unit, where], to)
        return away, pltpu.make_async_copy(source, target, third_recv.at[unit, where])

    def reduce(unit):
        axis = UNITS[unit][2]
        slots = 8 if axis == "y" else 16
        source = sums_y_ref.at[unit - 2] if axis == "y" else sums_ref.at[unit]

        def run():
            for o in range(16):
                pltpu.make_async_copy(source.at[o], source.at[o], second_recv.at[unit, o]).wait()
            for row in range(STRIP):
                total = source[0, row]
                for o in range(1, 16):
                    total = total + source[o, row]
                final_ref[unit, pl.ds(row, slots, stride=STRIP), :] = total
            for o, to, at, own in third_copies(unit):
                away, home = third_refs(unit, o, to, at)
                if own is True:
                    home.start()
                elif own is False:
                    away.start()
                else:
                    pl.when(own)(home.start)
                    pl.when(jnp.logical_not(own))(away.start)

        if axis == "y":
            run()
        else:
            pl.when(here.odd == 0)(run)

    def end_third(unit):
        def run():
            for o, to, at, own in third_copies(unit):
                away, _ = third_refs(unit, o, to, at)
                if own is True:
                    continue
                if own is False:
                    away.wait_send()
                else:
                    pl.when(jnp.logical_not(own))(away.wait_send)

        if UNITS[unit][2] == "y":
            run()
        else:
            pl.when(here.odd == 0)(run)

    def finish(unit):
        array, half, _ = UNITS[unit]
        out_ref = weighted_ref if array else weight_ref
        for step in range(SIDE):
            part = got_final_ref.at[unit, step]
            pltpu.make_async_copy(part, part, third_recv.at[unit, step]).wait()
            rows = slice(half * TILE + step * STRIP, half * TILE + (step + 1) * STRIP)
            out_ref[rows, :BLOCK] = got_final_ref[unit, step, :STRIP, :]
            out_ref[rows, BLOCK:] = got_final_ref[unit, step, STRIP:, :]

    compute(0)
    for at in range(3):
        take_slots(at)
    gather(0)
    gather(1)
    compute(1)
    gather(2)
    reduce(0)
    reduce(1)
    gather(3)
    reduce(2)
    finish(0)
    finish(1)
    reduce(3)
    finish(2)
    finish(3)
    for at in range(3):
        for o in range(1, 8):
            slots_copy(at, o).wait_send()
    for unit in range(4):
        for o in range(1, 8):
            first_copy(unit, o, everything).wait_send()
        end_second(unit)
        end_third(unit)


def fused(count, quadrants, pixels, variances, rows, coefs, meta):
    vmem = pl.BlockSpec(memory_space=pltpu.VMEM)
    smem = pl.BlockSpec(memory_space=pltpu.SMEM)
    dma = pltpu.SemaphoreType.DMA
    f32, bf16 = jnp.float32, jnp.bfloat16
    units = len(UNITS)
    return pl.pallas_call(
        fused_kernel,
        out_shape=(jax.ShapeDtypeStruct((64, 256), f32),) * 2,
        in_specs=[smem, smem] + [vmem] * 5,
        out_specs=(vmem, vmem),
        scratch_shapes=[
            pltpu.VMEM((NB * TILE, 256), bf16),
            pltpu.VMEM((NB, 256, 256), bf16),
            pltpu.VMEM((BLOCKS, 3, NB, BLOCK), f32),
            pltpu.VMEM((NB, GROUP * TILE, 256), bf16),
            pltpu.VMEM((units * 8, SLAB, BLOCK), f32),
            pltpu.VMEM((3, 8, 256), jnp.int32),
            pltpu.VMEM((24, 8, 256), jnp.int32),
            pltpu.VMEM((units * 8, SLAB, BLOCK), f32),
            pltpu.VMEM((units, STRIP, SLOTS, BLOCK), f32),
            pltpu.VMEM((2, 16, STRIP, 8, BLOCK), f32),
            pltpu.VMEM((2, 16, STRIP, 16, BLOCK), f32),
            pltpu.VMEM((units, 16 * STRIP, BLOCK), f32),
            pltpu.VMEM((units, SIDE, 2 * STRIP, BLOCK), f32),
            dma((3, 8)), dma((3, 8)),
            dma((units, 8)), dma((units, 8)),
            dma((units, 16)), dma((units, 16)),
            dma((units, 8)), dma((units, SIDE)),
        ],
        compiler_params=pltpu.CompilerParams(collective_id=0, has_side_effects=True, vmem_limit_bytes=56 << 20),
        name="coadd",
    )(count, quadrants, pixels, variances, rows, coefs, meta)


def on_device(
    image, variance, dest_patch, quadrant, coef_index, block_count, coef_table, row_taps, col_taps
):
    live = (jnp.arange(BLOCKS) < block_count[0, 0]).astype(jnp.int32)
    meta = jnp.stack([dest_patch[0, 0], quadrant[0, 0], live] + [live] * 5)
    meta = jnp.tile(meta, (1, 256 // BLOCKS))
    coefs = jnp.take(coef_table, coef_index[0, 0], axis=0)
    weighted, weight = fused(
        block_count[0], quadrant[0, 0], image[0, 0], variance[0, 0], tap_rows(row_taps, col_taps), coefs, meta
    )
    return weighted[None], weight[None]


def solution(mesh):
    placed = (
        P("visit", "patch", None, None, None),
        P("visit", "patch", None, None, None),
        P("visit", "patch", None),
        P("visit", "patch", None),
        P("visit", "patch", None),
        P("visit", "patch"),
        P(),
        P(),
        P(),
    )
    return jax.shard_map(
        on_device,
        mesh=mesh,
        in_specs=placed,
        out_specs=(P("patch", "visit", None), P("patch", "visit", None)),
        check_vma=False,
    )
```

time: 250 us -> 81.6 us (0.33)
  waiting for transfers between devices: 61.8 us -> 0 us
  blocking collectives: 58.1 us -> 0 us
  Pallas kernels: 20.3 us -> 69.7 us
  local copies, waits for them, and re-layouts: 42.5 us -> 8.72 us
  other arithmetic: 31 us -> 1.54 us
  starting transfers between devices: 14.4 us -> 0 us
  between operations: 15.3 us -> 1.38 us
  matrix products: 4.53 us -> 0 us
    all_to_all x1 -> x0, blocking collectives: 58.1 us -> none  [on_device(): send(slot_inverse)]
    pallas_call x1, Pallas kernels: 20.3 us -> 69.7 us  [fused(): pl.pallas_call(fused_kernel, out_shape=(jax.ShapeDtypeStruct((64, 256), f...]
    all_to_all x2 -> x0, waiting for transfers between devices: 42.4 us -> none  [the longest x1 42.4 us: on_device(): send(slot_weighted)]
    reduce_scatter x2 -> x0, waiting for transfers between devices: 19.4 us -> none  [on_device(): lax.psum_scatter(patch, 'visit', scatter_dimension=0, tiled=True)[None]]
    all_to_all x2 -> x0, starting transfers between devices: 14.1 us -> none  [the longest x1 9.49 us: on_device(): got_quarter = send(slot_quarter).reshape(-1, 2, 2)]
    all_to_all x2 -> x0, local copies, waits for them, and re-layouts: 10.9 us -> none  [the longest x1 5.43 us: on_device(): send(slot_inverse)]
    convert_element_type x49 -> x1, other arithmetic: 10.3 us -> 0.01 us  [on_device(): live = (jnp.arange(BLOCKS) < block_count[0, 0]).astype(jnp.int32)]
    mul x3 -> x0, other arithmetic: 9.83 us -> none  [the longest x1 8.56 us: on_device(): jnp.take(inverse, source, axis=0) * presence[:, None, None]]
  transfers between devices with their start and end apart: 4 -> 0, of which waited for: 2 -> 0; matrix products, arithmetic and copies ran while one was open for 29% -> 0% of each run, Pallas kernels for 8% -> 0%
where the time goes in v2:
time: 81.6 us; the launch traced here: 81.3 us
  Pallas kernels  69.7 us (85%)
  local copies, waits for them, and re-layouts  8.72 us (11%)
  other arithmetic  1.54 us (2%)
  between operations  1.38 us (2%)
    pallas_call x1, Pallas kernels, fused(): pl.pallas_call(fused_kernel, out_shape=(jax.ShapeDtypeStruct((64, 256), f...  69.7 us
    unnamed x9, local copies, waits for them, and re-layouts  5.54 us

profile of v2, /device:TPU:1, one launch (start us, length us, event | category | flops | bytes accessed | tf_op | source)
XLA Modules:
  0.0 81.3 jit_solution(9158809399289496154)
XLA Ops:
  0.6 0.0 copy-start
  0.6 0.0 copy-start.2
  0.7 0.0 copy-start.1
  1.3 0.8 rev.3
  2.1 0.7 subtract_reduce-precision_fusion
  2.8 0.1 slice.18
  2.9 0.1 slice.20
  3.0 0.7 concatenate.3.rows_ref
  3.7 2.6 %copy.11 = f32[800,16,6]{1,2,0:T(8,128)S(1)} copy(f32[800,16,6]{0,1,2:T(8,128)} %param.15) | data formatting | bytes 614400 | tf_op args[6]
  6.2 0.0 copy-done.2
  6.3 0.6 gather_fusion
  6.9 0.3 copy.12
  7.1 0.8 broadcast_select_fusion.coef_ref
  8.0 0.0 copy-done
  8.0 0.0 copy-done.1
  8.0 0.7 tile.10.meta_ref
  8.7 69.7 %coadd.1 = (f32[64,256]{1,0:T(8,128)}, f32[64,256]{1,0:T(8,128)}) custom-call(s32[1]{0:T(128)} %bitcast.17.count_ref, s32[32]{0:T(128)} %bitcast.25, f32[32,128,128]{2,1,0:T(8,128)} %bitcast.19, f32[32,128,128]{2,1,0:T(8,128)} %bitcast.20, f32[16,512]{1,0:T(8,128)} %concatenate.3.rows_ref, f32[32,16,6]{2,1,0:T(8,128)} %broadcast_select_fusion.coef_ref, ...), custom_call_target="tpu_custom_call" | custom-call | tf_op jit(solution)/shard_map/coadd/pallas_call | solution.py:432
  78.3 1.5 %copy.16 = f32[1,64,256]{2,1,0:T(8,128)} copy(f32[1,64,256]{2,1,0:T(8,128)} %bitcast.24) | data formatting | bytes 131072
  79.8 1.5 %copy.17 = f32[1,64,256]{2,1,0:T(8,128)} copy(f32[1,64,256]{2,1,0:T(8,128)} %bitcast.23) | data formatting | bytes 131072
  (11 shorter events, 0.1 us)
Async XLA Ops:
  0.6 7.3 %copy-start = (s32[1,1,32]{2,1,0:T(1,128)S(1)}, s32[1,1,32]{2,1,0:T(1,128)}, u32[]{:S(2)}) copy-start(s32[1,1,32]{2,1,0:T(1,128)} %param.12) | copy-start | bytes 388
  0.6 5.6 %copy-start.2 = (s32[1,1,32]{2,1,0:T(1,128)S(1)}, s32[1,1,32]{2,1,0:T(1,128)}, u32[]{:S(2)}) copy-start(s32[1,1,32]{2,1,0:T(1,128)} %param.13) | copy-start | bytes 388
  0.7 7.3 %copy-start.1 = (s32[1,1,32]{2,1,0:T(1,128)S(1)}, s32[1,1,32]{2,1,0:T(1,128)}, u32[]{:S(2)}) copy-start(s32[1,1,32]{2,1,0:T(1,128)} %param.11) | copy-start | bytes 388

commit v3 on v2

--- a/solution.py
+++ b/solution.py
@@ -1,4 +1,3 @@
-import functools
 import itertools
 
 import jax
@@ -22,7 +21,7 @@
 SLOTS = 128
 SLAB = BLOCKS * STRIP
 MESH = pl.DeviceIdType.MESH
-UNITS = ((0, 0, "x"), (0, 1, "z"), (1, 0, "y"), (1, 1, "y"))
+UNITS = ((0, 0, "x", "zy"), (0, 1, "z", "yx"), (1, 0, "y", "zx"), (1, 1, "x", "plane"))
 AXES = ("x", "y", "z")
 
 
@@ -31,30 +30,19 @@
     return high, (x - high.astype(jnp.float32)).astype(jnp.bfloat16)
 
 
-def tap_rows(row_taps, col_taps):
-    def parts(x):
-        high = lax.reduce_precision(x, exponent_bits=8, mantissa_bits=7)
-        return high, lax.reduce_precision(x - high, exponent_bits=8, mantissa_bits=7)
-
-    def zeros(width):
-        return jnp.zeros((NB, width), jnp.float32)
-
-    high, low = parts(col_taps[:, ::-1])
-    gap = zeros(WIN - TAPS)
-    lead = LEAD - REACH
-    row_high, row_low = parts(row_taps)
-    around = zeros(BLOCK - TAPS)
-    return jnp.concatenate(
-        [
-            zeros(lead), high, gap, low, gap, high, zeros(256 - 2 * WIN - lead - TAPS),
-            row_high[:, REACH:], around, row_high[:, :REACH],
-            row_low[:, REACH:], around, row_low[:, :REACH],
-        ],
-        axis=1,
-    )
-
-
-def build_bands(rows_ref, left_ref, right_ref):
+def build_bands(row_ref, col_ref, left_ref, right_ref):
+    tap = lax.broadcasted_iota(jnp.int32, (TAPS, 256), 0)
+    lane = lax.broadcasted_iota(jnp.int32, (TAPS, 256), 1)
+
+    def place(parts, *found):
+        hot = [f.astype(jnp.float32).astype(jnp.bfloat16) for f in found]
+        return sum(jnp.dot(p, h, preferred_element_type=jnp.float32) for p, h in zip(parts, hot))
+
+    at = LEAD + REACH - tap
+    spread_rows = place(split(col_ref[...]), (lane == at) | (lane == at + 2 * WIN), lane == at + WIN)
+    at = lax.rem(tap + (BLOCK - REACH), BLOCK)
+    high, low = split(row_ref[...])
+    row_high, row_low = place((high,), lane == at)[:, :BLOCK], place((low,), lane == at)[:, :BLOCK]
     near = lax.broadcasted_iota(jnp.int32, (BLOCK, BLOCK), 1) - lax.broadcasted_iota(jnp.int32, (BLOCK, BLOCK), 0)
     near = (near <= REACH) & (near >= -REACH)
 
@@ -62,35 +50,39 @@
         return pltpu.roll(jnp.broadcast_to(row, (height, row.shape[1])), 0, 1, stride=1, stride_axis=0)
 
     for k in range(NB):
-        band = roll(rows_ref[k : k + 1, :256], TILE)
+        band = roll(spread_rows[k : k + 1, :], TILE)
         left_ref[k * TILE : (k + 1) * TILE, :] = band.astype(jnp.bfloat16)
-        high = jnp.where(near, roll(rows_ref[k : k + 1, 256 : 256 + BLOCK], BLOCK), 0.0).astype(jnp.bfloat16)
-        low = jnp.where(near, roll(rows_ref[k : k + 1, 256 + BLOCK :], BLOCK), 0.0).astype(jnp.bfloat16)
+        high = jnp.where(near, roll(row_high[k : k + 1, :], BLOCK), 0.0).astype(jnp.bfloat16)
+        low = jnp.where(near, roll(row_low[k : k + 1, :], BLOCK), 0.0).astype(jnp.bfloat16)
         right_ref[k, :BLOCK, :BLOCK] = high
         right_ref[k, :BLOCK, BLOCK:] = low
         right_ref[k, BLOCK:, :BLOCK] = high
         right_ref[k, BLOCK:, BLOCK:] = jnp.zeros_like(low)
 
 
-def build_polynomials(coef_ref, quadrant_ref, poly_ref):
+def build_polynomials(table_ref, index_ref, quadrant_ref, poly_ref):
+    entry = lax.broadcasted_iota(jnp.int32, (table_ref.shape[1], BLOCK), 0)
+    index = jnp.concatenate([index_ref[...]] * (BLOCK // BLOCKS), axis=1)
+    hot = (entry == index).astype(jnp.float32).astype(jnp.bfloat16)
+    rest, coefs = table_ref[...], None
+    for _ in range(3):
+        part = rest.astype(jnp.bfloat16)
+        rest = rest - part.astype(jnp.float32)
+        picked = jnp.dot(part, hot, preferred_element_type=jnp.float32)
+        coefs = picked if coefs is None else coefs + picked
     column = lax.broadcasted_iota(jnp.int32, (NB, BLOCK), 1).astype(jnp.float32)
     own = (column + 0.5) / BLOCK - 1.0
-
-    def build(b, carry):
+    for b in range(BLOCKS):
         quadrant = quadrant_ref[b]
         down = (quadrant // 2).astype(jnp.float32)
         u = own + (quadrant % 2).astype(jnp.float32)
-        a = coef_ref[b]
-        a = [jnp.broadcast_to(a[:, m : m + 1], (NB, BLOCK)) for m in range(6)]
+        a = [jnp.broadcast_to(coefs[m * NB : (m + 1) * NB, b : b + 1], (NB, BLOCK)) for m in range(6)]
         q = a[0] + u * (a[1] + u * a[3])
         s = a[2] + u * a[4]
         e = a[5]
         poly_ref[b, 0] = q + down * (s + down * e)
         poly_ref[b, 1] = s + (2.0 * down) * e
         poly_ref[b, 2] = e
-        return carry
-
-    lax.fori_loop(0, BLOCKS, build, 0)
 
 
 def window(image_ref, block, tile):
@@ -164,24 +156,30 @@
     return sorted(found)
 
 
-def slot_rows(meta_ref, axis, here):
-    patch, quadrant, live = meta_ref[0:1, :], meta_ref[1:2, :], meta_ref[2:3, :]
-    x, z, c = lax.div(patch, 8), lax.rem(lax.div(patch, 2), 4), lax.rem(patch, 2)
+def slot_rows(patches, quadrants, live, unit, here):
+    _, _, axis, later = UNITS[unit]
+    patch, quadrant = (jnp.concatenate([ref[...]] * 8, axis=1) for ref in (patches, quadrants))
+    part = {"x": lax.div(patch, 8), "z": lax.rem(lax.div(patch, 2), 4)}
+    sizes = {"x": 4, "z": 4, "y": 2}
+    c = lax.rem(patch, 2)
     down, across = lax.div(quadrant, 2), lax.rem(quadrant, 2)
+    part["y"] = down
+    order = later if later != "plane" else "".join(a for a in "xzy" if a != axis)
+    slot = part[order[0]] * sizes[order[1]] + part[order[1]]
     if axis == "y":
-        slot = (x * 4 + z) * 8 + c * 4 + down * 2 + across
-    elif axis == "x":
-        slot = (z * 2 + down) * 16 + (x * 2 + c) * 2 + across
+        slot = slot * 8 + c * 4 + down * 2 + across
     else:
-        slot = (x * 2 + down) * 16 + (z * 2 + c) * 2 + across
+        slot = slot * 16 + part[axis] * 4 + c * 2 + across
     lane = lax.broadcasted_iota(jnp.int32, slot.shape, 1)
-    mine = (lane >= here.strip(axis) * BLOCKS) & (lane < here.strip(axis) * BLOCKS + BLOCKS) & (live > 0)
+    at = lane - here.strip(axis) * BLOCKS
+    mine = (at >= 0) & (at < jnp.minimum(live, BLOCKS))
     return jnp.broadcast_to(jnp.where(mine, slot, -1), (8, 256))
 
 
 def fused_kernel(
-    count_ref, quadrant_ref, image_ref, variance_ref, rows_ref, coef_ref, meta_ref, weighted_ref, weight_ref,
-    left_ref, right_ref, poly_ref, parts_ref, strips_ref, slots_ref, got_slots_ref, got_ref, dense_ref, sums_y_ref, sums_ref,
+    count_ref, quadrant_ref, image_ref, variance_ref, row_ref, col_ref, table_ref, index_ref, patches_ref, quadrants_ref,
+    out_ref,
+    left_ref, right_ref, poly_ref, parts_ref, strips_ref, slots_ref, got_slots_ref, got_ref, dense_ref, near_ref, middle_ref, far_ref, sums_ref,
     final_ref, got_final_ref,
     slots_send, slots_recv, first_send, first_recv, second_send, second_recv, third_send, third_recv,
 ):
@@ -202,8 +200,8 @@
         return carry
 
     lax.fori_loop(0, BLOCKS, invert, 0)
-    for at, axis in enumerate(AXES):
-        slots_ref[at] = slot_rows(meta_ref, axis, here)
+    for unit in range(4):
+        slots_ref[unit] = slot_rows(patches_ref, quadrants_ref, live, unit, here)
     pl.semaphore_wait(barrier, len(all_partners))
 
     def remote(src, dst, send, recv, to):
@@ -211,13 +209,9 @@
             src_ref=src, dst_ref=dst, send_sem=send, recv_sem=recv, device_id=to["id"], device_id_type=MESH
         )
 
-    def slots_copy(at, o):
-        to = here.at(c=o % 2, **{AXES[at]: o // 2})
-        return remote(slots_ref.at[at], got_slots_ref.at[at * 8 + o], slots_send.at[at, o], slots_recv.at[at, o], to)
-
-    for at in range(3):
-        for o in range(1, 8):
-            slots_copy(at, o).start()
+    def slots_copy(unit, o):
+        to = here.at(c=o % 2, **{UNITS[unit][2]: o // 2})
+        return remote(slots_ref.at[unit], got_slots_ref.at[unit * 8 + o], slots_send.at[unit, o], slots_recv.at[unit, o], to)
 
     def first_copy(unit, o, rows):
         axis = UNITS[unit][2]
@@ -232,11 +226,14 @@
     for unit in range(2):
         for o in range(8):
             first_copy(unit, o, everything).start()
-
-    build_bands(rows_ref, left_ref, right_ref)
-    build_polynomials(coef_ref, quadrant_ref, poly_ref)
-
-    def compute(half):
+    for unit in range(4):
+        for o in range(1, 8):
+            slots_copy(unit, o).start()
+
+    build_bands(row_ref, col_ref, left_ref, right_ref)
+    build_polynomials(table_ref, index_ref, quadrant_ref, poly_ref)
+
+    def compute(half, begin, end):
         unit = 2 + half
 
         def step(group, carry):
@@ -257,60 +254,130 @@
                 first_copy(unit, o, rows).start()
             return carry
 
-        lax.fori_loop(0, BLOCKS // GROUP, step, 0)
-
-    def take_slots(at):
+        lax.fori_loop(begin, end, step, 0)
+
+    def take_slots(unit):
         for o in range(1, 8):
-            slots_copy(at, o).wait_recv()
-
-    def second_copies(unit):
-        axis = UNITS[unit][2]
-        if axis == "y":
-            for o in range(16):
-                to = here.at(x=o // 4, z=o % 4)
-                base = pl.multiple_of((to["x"] * SIDE + to["z"]) * 8, 8)
-                yield o, to, dense_ref.at[unit, :, pl.ds(base, 8), :], sums_y_ref.at[unit - 2, o], o, o == 0
-        else:
-            other = "z" if axis == "x" else "x"
-            for o in range(8):
-                rise = here.odd + 2 * (o % 2)
-                to = here.at(**{other: o // 2, "y": rise})
-                base = pl.multiple_of((to[other] * 2 + lax.div(to["y"], 2)) * 16, 16)
-                where = (o // 2) * 4 + rise
-                yield o, to, dense_ref.at[unit, :, pl.ds(base, 16), :], sums_ref.at[unit, where], where, here.odd == 0 if o == 0 else False
+            slots_copy(unit, o).wait_recv()
+
+    def choose(own, home, away):
+        if own is True:
+            home()
+        elif own is False:
+            away()
+        else:
+            pl.when(own)(home)
+            pl.when(jnp.logical_not(own))(away)
+
+    def nothing():
+        pass
+
+    def halved(unit, axis):
+        return axis == "y" and UNITS[unit][2] != "y"
+
+    def steps(unit, axis):
+        if halved(unit, axis):
+            for m in range(2):
+                rise = here.odd + 2 * m
+                to = here.at(y=rise)
+                yield rise, to, lax.div(to["y"], 2), (here.odd == 0 if m == 0 else False)
+        else:
+            for o in range(SIDE):
+                to = here.at(**{axis: o})
+                yield o, to, to[axis], o == 0
+
+    def width(unit):
+        return 8 if UNITS[unit][2] == "y" else 16
+
+    def line(unit, second):
+        axis = UNITS[unit][3][second]
+        slots = width(unit)
+        if not second:
+            slots = slots * (2 if halved(unit, UNITS[unit][3][1]) else SIDE)
+        source, target = (middle_ref, far_ref) if second else (dense_ref, near_ref)
+        for at, (o, to, share, own) in enumerate(steps(unit, axis)):
+            part = source.at[unit, :, pl.ds(pl.multiple_of(share * slots, 8), slots), :]
+            place = target.at[unit, o, :, pl.ds(0, slots), :]
+            arrived = second_recv.at[unit, 4 * second + o]
+            yield (
+                pltpu.make_async_copy(part, place, arrived) if own is not False else None,
+                remote(part, place, second_send.at[unit, 4 * second + at], arrived, to) if own is not True else None,
+                own,
+            )
+
+    def plane(unit):
+        slots = width(unit)
+        first, last = (a for a in "xzy" if a != UNITS[unit][2])
+        for at, ((o, to, share, own), (p, on, more, also)) in enumerate(
+            itertools.product(steps(unit, first), steps(unit, last))
+        ):
+            to = dict(to, **{last: on[last]})
+            to["id"] = (to["y"], (to["x"] * SIDE + to["z"]) * 2 + to["c"])
+            base = pl.multiple_of((share * (2 if halved(unit, last) else SIDE) + more) * slots, 8)
+            part = dense_ref.at[unit, :, pl.ds(base, slots), :]
+            place = sums_ref.at[o * SIDE + p, :, pl.ds(0, slots), :]
+            arrived = second_recv.at[unit, o * SIDE + p]
+            own = False if own is False or also is False else also if own is True else own
+            yield (
+                pltpu.make_async_copy(part, place, arrived) if own is not False else None,
+                remote(part, place, second_send.at[unit, at], arrived, to) if own is not True else None,
+                own,
+            )
+
+    def start_all(copies):
+        for home, away, own in copies:
+            choose(own, home and home.start, away and away.start)
+
+    def end_all(copies):
+        for home, away, own in copies:
+            choose(own, nothing, away and away.wait_send)
 
     def start_second(unit):
-        for o, to, source, target, where, own in second_copies(unit):
-            away = remote(source, target, second_send.at[unit, o], second_recv.at[unit, where], to)
-            home = pltpu.make_async_copy(source, target, second_recv.at[unit, where])
-            if own is True:
-                home.start()
-            elif own is False:
-                away.start()
-            else:
-                pl.when(own)(home.start)
-                pl.when(jnp.logical_not(own))(away.start)
+        start_all(plane(unit) if UNITS[unit][3] == "plane" else line(unit, 0))
+
+    def arrived_sum(source, slots, unit, sems):
+        for n, at in enumerate(sems):
+            part = source.at[n, :, pl.ds(0, slots), :]
+            pltpu.make_async_copy(part, part, second_recv.at[unit, at]).wait()
+
+    def where_owner(unit, axis, run):
+        if halved(unit, axis):
+            pl.when(here.odd == 0)(run)
+        else:
+            run()
+
+    def pass_on(unit):
+        first, last = UNITS[unit][3]
+        slots = width(unit) * (2 if halved(unit, last) else SIDE)
+
+        def run():
+            arrived_sum(near_ref.at[unit], slots, unit, range(4))
+            for row in range(STRIP):
+                total = near_ref[unit, 0, row, :slots, :]
+                for o in range(1, SIDE):
+                    total = total + near_ref[unit, o, row, :slots, :]
+                middle_ref[unit, row, :slots, :] = total
+            start_all(line(unit, 1))
+
+        where_owner(unit, first, run)
 
     def end_second(unit):
-        for o, to, source, target, where, own in second_copies(unit):
-            away = remote(source, target, second_send.at[unit, o], second_recv.at[unit, where], to)
-            if own is True:
-                continue
-            if own is False:
-                away.wait_send()
-            else:
-                pl.when(jnp.logical_not(own))(away.wait_send)
+        if UNITS[unit][3] == "plane":
+            end_all(plane(unit))
+        else:
+            end_all(line(unit, 0))
+            where_owner(unit, UNITS[unit][3][0], lambda: end_all(line(unit, 1)))
 
     def gather(unit):
-        axis = UNITS[unit][2]
         for o in range(8):
             if o == 0:
                 first_copy(unit, 0, everything).wait()
             else:
                 first_copy(unit, o, everything).wait_recv()
-        slots = slots_ref[AXES.index(axis)]
+        take_slots(unit)
+        slots = slots_ref[unit]
         for o in range(1, 8):
-            slots = jnp.maximum(slots, got_slots_ref[AXES.index(axis) * 8 + o])
+            slots = jnp.maximum(slots, got_slots_ref[unit * 8 + o])
         hot = lax.broadcasted_iota(jnp.int32, (SLOTS, 256), 0) == slots[0:1, :]
         hot = hot.astype(jnp.float32).astype(jnp.bfloat16)
         for row in range(STRIP):
@@ -345,16 +412,18 @@
 
     def reduce(unit):
         axis = UNITS[unit][2]
-        slots = 8 if axis == "y" else 16
-        source = sums_y_ref.at[unit - 2] if axis == "y" else sums_ref.at[unit]
+        slots = width(unit)
 
         def run():
-            for o in range(16):
-                pltpu.make_async_copy(source.at[o], source.at[o], second_recv.at[unit, o]).wait()
+            if UNITS[unit][3] == "plane":
+                source, sems = sums_ref, range(16)
+            else:
+                source, sems = far_ref.at[unit], range(4, 8)
+            arrived_sum(source, slots, unit, sems)
             for row in range(STRIP):
-                total = source[0, row]
-                for o in range(1, 16):
-                    total = total + source[o, row]
+                total = source[0, row, :slots, :]
+                for o in range(1, len(sems)):
+                    total = total + source[o, row, :slots, :]
                 final_ref[unit, pl.ds(row, slots, stride=STRIP), :] = total
             for o, to, at, own in third_copies(unit):
                 away, home = third_refs(unit, o, to, at)
@@ -388,42 +457,42 @@
             pl.when(here.odd == 0)(run)
 
     def finish(unit):
-        array, half, _ = UNITS[unit]
-        out_ref = weighted_ref if array else weight_ref
+        array, half = UNITS[unit][:2]
         for step in range(SIDE):
             part = got_final_ref.at[unit, step]
             pltpu.make_async_copy(part, part, third_recv.at[unit, step]).wait()
             rows = slice(half * TILE + step * STRIP, half * TILE + (step + 1) * STRIP)
-            out_ref[rows, :BLOCK] = got_final_ref[unit, step, :STRIP, :]
-            out_ref[rows, BLOCK:] = got_final_ref[unit, step, STRIP:, :]
-
-    compute(0)
-    for at in range(3):
-        take_slots(at)
+            out_ref[array, rows, :BLOCK] = got_final_ref[unit, step, :STRIP, :]
+            out_ref[array, rows, BLOCK:] = got_final_ref[unit, step, STRIP:, :]
+
+    compute(0, 0, 4)
     gather(0)
     gather(1)
-    compute(1)
+    compute(1, 0, 2)
+    pass_on(0)
+    pass_on(1)
     gather(2)
+    compute(1, 2, 4)
+    pass_on(2)
     reduce(0)
     reduce(1)
     gather(3)
     reduce(2)
     finish(0)
     finish(1)
+    finish(2)
     reduce(3)
-    finish(2)
     finish(3)
-    for at in range(3):
+    for unit in range(4):
         for o in range(1, 8):
-            slots_copy(at, o).wait_send()
-    for unit in range(4):
+            slots_copy(unit, o).wait_send()
         for o in range(1, 8):
             first_copy(unit, o, everything).wait_send()
         end_second(unit)
         end_third(unit)
 
 
-def fused(count, quadrants, pixels, variances, rows, coefs, meta):
+def fused(count, quadrants, *arrays):
     vmem = pl.BlockSpec(memory_space=pltpu.VMEM)
     smem = pl.BlockSpec(memory_space=pltpu.SMEM)
     dma = pltpu.SemaphoreType.DMA
@@ -431,44 +500,44 @@
     units = len(UNITS)
     return pl.pallas_call(
         fused_kernel,
-        out_shape=(jax.ShapeDtypeStruct((64, 256), f32),) * 2,
-        in_specs=[smem, smem] + [vmem] * 5,
-        out_specs=(vmem, vmem),
+        out_shape=jax.ShapeDtypeStruct((2, 64, 256), f32),
+        in_specs=[smem, smem] + [vmem] * len(arrays),
+        out_specs=vmem,
         scratch_shapes=[
             pltpu.VMEM((NB * TILE, 256), bf16),
             pltpu.VMEM((NB, 256, 256), bf16),
             pltpu.VMEM((BLOCKS, 3, NB, BLOCK), f32),
             pltpu.VMEM((NB, GROUP * TILE, 256), bf16),
             pltpu.VMEM((units * 8, SLAB, BLOCK), f32),
-            pltpu.VMEM((3, 8, 256), jnp.int32),
-            pltpu.VMEM((24, 8, 256), jnp.int32),
+            pltpu.VMEM((units, 8, 256), jnp.int32),
+            pltpu.VMEM((units * 8, 8, 256), jnp.int32),
             pltpu.VMEM((units * 8, SLAB, BLOCK), f32),
             pltpu.VMEM((units, STRIP, SLOTS, BLOCK), f32),
-            pltpu.VMEM((2, 16, STRIP, 8, BLOCK), f32),
-            pltpu.VMEM((2, 16, STRIP, 16, BLOCK), f32),
+            pltpu.VMEM((units, SIDE, STRIP, 64, BLOCK), f32),
+            pltpu.VMEM((units, STRIP, 64, BLOCK), f32),
+            pltpu.VMEM((units, SIDE, STRIP, 16, BLOCK), f32),
+            pltpu.VMEM((16, STRIP, 16, BLOCK), f32),
             pltpu.VMEM((units, 16 * STRIP, BLOCK), f32),
             pltpu.VMEM((units, SIDE, 2 * STRIP, BLOCK), f32),
-            dma((3, 8)), dma((3, 8)),
+            dma((units, 8)), dma((units, 8)),
             dma((units, 8)), dma((units, 8)),
             dma((units, 16)), dma((units, 16)),
             dma((units, 8)), dma((units, SIDE)),
         ],
         compiler_params=pltpu.CompilerParams(collective_id=0, has_side_effects=True, vmem_limit_bytes=56 << 20),
         name="coadd",
-    )(count, quadrants, pixels, variances, rows, coefs, meta)
+    )(count, quadrants, *arrays)
 
 
 def on_device(
     image, variance, dest_patch, quadrant, coef_index, block_count, coef_table, row_taps, col_taps
 ):
-    live = (jnp.arange(BLOCKS) < block_count[0, 0]).astype(jnp.int32)
-    meta = jnp.stack([dest_patch[0, 0], quadrant[0, 0], live] + [live] * 5)
-    meta = jnp.tile(meta, (1, 256 // BLOCKS))
-    coefs = jnp.take(coef_table, coef_index[0, 0], axis=0)
-    weighted, weight = fused(
-        block_count[0], quadrant[0, 0], image[0, 0], variance[0, 0], tap_rows(row_taps, col_taps), coefs, meta
+    table = coef_table.transpose(2, 1, 0).reshape(-1, coef_table.shape[0])
+    sums = fused(
+        block_count[0], quadrant[0, 0], image[0, 0], variance[0, 0], row_taps, col_taps, table,
+        coef_index[0], dest_patch[0], quadrant[0],
     )
-    return weighted[None], weight[None]
+    return sums[1][None], sums[0][None]
 
 
 def solution(mesh):

time: 81.6 us -> 65.5 us (0.80)
  Pallas kernels: 69.7 us -> 62.5 us
  local copies, waits for them, and re-layouts: 8.72 us -> 1.53 us
  other arithmetic: 1.54 us -> 0 us
    pallas_call x1, Pallas kernels: 69.7 us -> 62.5 us  [fused(): pl.pallas_call(fused_kernel, out_shape=jax.ShapeDtypeStruct((2, 64, 256),...]
    unnamed x9 -> x0, local copies, waits for them, and re-layouts: 5.54 us -> none
    slice x2 -> x1, local copies, waits for them, and re-layouts: 0.14 us -> 1.53 us  [on_device(): return (sums[1][None], sums[0][None])]
    gather x2 -> x0, local copies, waits for them, and re-layouts: 0.85 us -> none  [on_device(): coefs = jnp.take(coef_table, coef_index[0, 0], axis=0)]
where the time goes in v3:
time: 65.5 us; the launch traced here: 65.3 us
  Pallas kernels  62.5 us (95%)
  local copies, waits for them, and re-layouts  1.53 us (2%)
  between operations  1.29 us (2%)
    pallas_call x1, Pallas kernels, fused(): pl.pallas_call(fused_kernel, out_shape=jax.ShapeDtypeStruct((2, 64, 256),...  62.5 us
    slice x1, local copies, waits for them, and re-layouts, on_device(): return (sums[1][None], sums[0][None])  1.53 us

profile of v3, /device:TPU:1, one launch (start us, length us, event | category | flops | bytes accessed | tf_op | source)
XLA Modules:
  0.0 65.3 jit_solution(10093328492738964016)
XLA Ops:
  1.3 62.5 %coadd.1 = f32[2,64,256]{2,1,0:T(8,128)} custom-call(s32[1]{0:T(128)} %bitcast.10.count_ref, s32[32]{0:T(128)} %bitcast.14, f32[32,128,128]{2,1,0:T(8,128)} %bitcast.11, f32[32,128,128]{2,1,0:T(8,128)} %bitcast.12, f32[16,41]{1,0:T(8,128)} %row_ref.1, f32[16,41]{1,0:T(8,128)} %col_ref.1, f32[96,800]{1,0:T(8,128)} %bitcast.13, s32[1,32]{1,0:T(1,128)} %bitcast.16, ...), custom_call_target="tpu_custom_call" | custom-call | tf_op jit(solution)/shard_map/coadd/pallas_call | solution.py:501
  63.8 1.5 %fusion = (f32[1,64,256]{2,1,0:T(8,128)}, f32[1,64,256]{2,1,0:T(8,128)}) fusion(f32[2,64,256]{2,1,0:T(8,128)} %coadd.1), kind=kLoop, calls=%fused_computation | loop fusion | bytes 262144 | tf_op jit(solution)/shard_map/slice | solution.py:540

commit v4 on v3

--- a/solution.py
+++ b/solution.py
@@ -177,9 +177,9 @@
 
 
 def fused_kernel(
-    count_ref, quadrant_ref, image_ref, variance_ref, row_ref, col_ref, table_ref, index_ref, patches_ref, quadrants_ref,
+    count_ref, quadrant_ref, image_hbm, variance_hbm, row_ref, col_ref, table_ref, index_ref, patches_ref, quadrants_ref,
     out_ref,
-    left_ref, right_ref, poly_ref, parts_ref, strips_ref, slots_ref, got_slots_ref, got_ref, dense_ref, near_ref, middle_ref, far_ref, sums_ref,
+    image_ref, variance_ref, load_sem, left_ref, right_ref, poly_ref, parts_ref, strips_ref, slots_ref, got_slots_ref, got_ref, dense_ref, near_ref, middle_ref, far_ref, sums_ref,
     final_ref, got_final_ref,
     slots_send, slots_recv, first_send, first_recv, second_send, second_recv, third_send, third_recv,
 ):
@@ -189,6 +189,14 @@
     for x, y, z, c in all_partners:
         pl.semaphore_signal(barrier, inc=1, device_id=here.at(x=x, y=y, z=z, c=c)["id"], device_id_type=MESH)
 
+    load_variance = pltpu.make_async_copy(variance_hbm, variance_ref, load_sem.at[0])
+    load_image = pltpu.make_async_copy(image_hbm, image_ref, load_sem.at[1])
+    load_variance.start()
+    load_image.start()
+    build_bands(row_ref, col_ref, left_ref, right_ref)
+    build_polynomials(table_ref, index_ref, quadrant_ref, poly_ref)
+    load_variance.wait()
+
     live = count_ref[0]
 
     def invert(b, carry):
@@ -229,11 +237,9 @@
     for unit in range(4):
         for o in range(1, 8):
             slots_copy(unit, o).start()
-
-    build_bands(row_ref, col_ref, left_ref, right_ref)
-    build_polynomials(table_ref, index_ref, quadrant_ref, poly_ref)
-
-    def compute(half, begin, end):
+    load_image.wait()
+
+    def compute(half, every, meanwhile):
         unit = 2 + half
 
         def step(group, carry):
@@ -249,12 +255,22 @@
                         )
 
                 matched_tile(core * 2 + half, first, image_ref, left_ref, right_ref, poly_ref, parts_ref, emit)
-            rows = pl.ds(pl.multiple_of(group * GROUP * STRIP, GROUP * STRIP), GROUP * STRIP)
-            for o in range(8):
-                first_copy(unit, o, rows).start()
+
+            def send():
+                size = every * GROUP * STRIP
+                rows = pl.ds(pl.multiple_of(lax.div(group, every) * size, size), size)
+                for o in range(8):
+                    first_copy(unit, o, rows).start()
+
+            if every == 1:
+                send()
+            else:
+                pl.when(lax.rem(group, every) == every - 1)(send)
+            for after, run in meanwhile:
+                pl.when(group == after)(run)
             return carry
 
-        lax.fori_loop(begin, end, step, 0)
+        lax.fori_loop(0, BLOCKS // GROUP, step, 0)
 
     def take_slots(unit):
         for o in range(1, 8):
@@ -465,22 +481,19 @@
             out_ref[array, rows, :BLOCK] = got_final_ref[unit, step, :STRIP, :]
             out_ref[array, rows, BLOCK:] = got_final_ref[unit, step, STRIP:, :]
 
-    compute(0, 0, 4)
-    gather(0)
-    gather(1)
-    compute(1, 0, 2)
-    pass_on(0)
-    pass_on(1)
-    gather(2)
-    compute(1, 2, 4)
-    pass_on(2)
-    reduce(0)
-    reduce(1)
+    def gather_inverses():
+        gather(0)
+        gather(1)
+
+    compute(0, 2, ())
+    compute(1, 1, ((1, gather_inverses), (2, lambda: gather(2))))
+    for unit in range(3):
+        pass_on(unit)
     gather(3)
-    reduce(2)
-    finish(0)
-    finish(1)
-    finish(2)
+    for unit in range(3):
+        reduce(unit)
+    for unit in range(3):
+        finish(unit)
     reduce(3)
     finish(3)
     for unit in range(4):
@@ -501,9 +514,12 @@
     return pl.pallas_call(
         fused_kernel,
         out_shape=jax.ShapeDtypeStruct((2, 64, 256), f32),
-        in_specs=[smem, smem] + [vmem] * len(arrays),
+        in_specs=[smem, smem] + [pl.BlockSpec(memory_space=pl.ANY)] * 2 + [vmem] * (len(arrays) - 2),
         out_specs=vmem,
         scratch_shapes=[
+            pltpu.VMEM((BLOCKS, BLOCK, BLOCK), f32),
+            pltpu.VMEM((BLOCKS, BLOCK, BLOCK), f32),
+            dma((2,)),
             pltpu.VMEM((NB * TILE, 256), bf16),
             pltpu.VMEM((NB, 256, 256), bf16),
             pltpu.VMEM((BLOCKS, 3, NB, BLOCK), f32),

time: 65.5 us -> 60.1 us (0.918)
  Pallas kernels: 62.5 us -> 57.1 us
    pallas_call x1, Pallas kernels: 62.5 us -> 57.1 us  [fused(): pl.pallas_call(fused_kernel, out_shape=jax.ShapeDtypeStruct((2, 64, 256),...]
where the time goes in v4:
time: 60.1 us; the launch traced here: 59.9 us
  Pallas kernels  57.1 us (95%)
  local copies, waits for them, and re-layouts  1.53 us (3%)
  between operations  1.29 us (2%)
    pallas_call x1, Pallas kernels, fused(): pl.pallas_call(fused_kernel, out_shape=jax.ShapeDtypeStruct((2, 64, 256),...  57.1 us
    slice x1, local copies, waits for them, and re-layouts, on_device(): return (sums[1][None], sums[0][None])  1.53 us

profile of v4, /device:TPU:1, one launch (start us, length us, event | category | flops | bytes accessed | tf_op | source)
XLA Modules:
  0.0 59.9 jit_solution(11736959553447356411)
XLA Ops:
  1.3 57.1 %coadd.1 = f32[2,64,256]{2,1,0:T(8,128)} custom-call(s32[1]{0:T(128)} %bitcast.10.count_ref, s32[32]{0:T(128)} %bitcast.14, f32[32,128,128]{2,1,0:T(8,128)} %bitcast.11, f32[32,128,128]{2,1,0:T(8,128)} %bitcast.12, f32[16,41]{1,0:T(8,128)} %row_ref.1, f32[16,41]{1,0:T(8,128)} %col_ref.1, f32[96,800]{1,0:T(8,128)} %bitcast.13, s32[1,32]{1,0:T(1,128)} %bitcast.16, ...), custom_call_target="tpu_custom_call" | custom-call | tf_op jit(solution)/shard_map/coadd/pallas_call | solution.py:514
  58.4 1.5 %fusion = (f32[1,64,256]{2,1,0:T(8,128)}, f32[1,64,256]{2,1,0:T(8,128)}) fusion(f32[2,64,256]{2,1,0:T(8,128)} %coadd.1), kind=kLoop, calls=%fused_computation | loop fusion | bytes 262144 | tf_op jit(solution)/shard_map/slice | solution.py:556

commit v5 on v4

--- a/solution.py
+++ b/solution.py
@@ -20,6 +20,7 @@
 SIDE = 4
 SLOTS = 128
 SLAB = BLOCKS * STRIP
+FULL = SLAB + STRIP
 MESH = pl.DeviceIdType.MESH
 UNITS = ((0, 0, "x", "zy"), (0, 1, "z", "yx"), (1, 0, "y", "zx"), (1, 1, "x", "plane"))
 AXES = ("x", "y", "z")
@@ -145,13 +146,14 @@
 
 def partners():
     found = set()
-    for axis in AXES:
-        others = [a for a in AXES if a != axis]
+    for _, _, axis, later in UNITS:
         for step, c in itertools.product(range(SIDE), range(2)):
             found.add(tuple(step if a == axis else 0 for a in AXES) + (c,))
+        others = [a for a in AXES if a != axis]
         for steps in itertools.product(range(SIDE), repeat=2):
-            to = dict(zip(others, steps))
-            found.add(tuple(to.get(a, 0) for a in AXES) + (0,))
+            if later == "plane" or 0 in steps:
+                to = dict(zip(others, steps))
+                found.add(tuple(to.get(a, 0) for a in AXES) + (0,))
     found.discard((0, 0, 0, 0))
     return sorted(found)
 
@@ -173,15 +175,17 @@
     lane = lax.broadcasted_iota(jnp.int32, slot.shape, 1)
     at = lane - here.strip(axis) * BLOCKS
     mine = (at >= 0) & (at < jnp.minimum(live, BLOCKS))
-    return jnp.broadcast_to(jnp.where(mine, slot, -1), (8, 256))
+    slot = jnp.broadcast_to(jnp.where(mine, slot, -1).astype(jnp.float32), (STRIP, 256))
+    row = lax.broadcasted_iota(jnp.int32, (STRIP, BLOCK), 0)
+    return jnp.where(row == 0, slot[:, :BLOCK], slot[:, BLOCK:])
 
 
 def fused_kernel(
     count_ref, quadrant_ref, image_hbm, variance_hbm, row_ref, col_ref, table_ref, index_ref, patches_ref, quadrants_ref,
     out_ref,
-    image_ref, variance_ref, load_sem, left_ref, right_ref, poly_ref, parts_ref, strips_ref, slots_ref, got_slots_ref, got_ref, dense_ref, near_ref, middle_ref, far_ref, sums_ref,
+    image_ref, variance_ref, load_sem, left_ref, right_ref, poly_ref, parts_ref, strips_ref, got_ref, dense_ref, near_ref, middle_ref, far_ref, sums_ref,
     final_ref, got_final_ref,
-    slots_send, slots_recv, first_send, first_recv, second_send, second_recv, third_send, third_recv,
+    first_send, first_recv, second_send, second_recv, third_send, third_recv,
 ):
     here = Here()
     barrier = pltpu.get_barrier_semaphore()
@@ -193,33 +197,27 @@
     load_image = pltpu.make_async_copy(image_hbm, image_ref, load_sem.at[1])
     load_variance.start()
     load_image.start()
-    build_bands(row_ref, col_ref, left_ref, right_ref)
-    build_polynomials(table_ref, index_ref, quadrant_ref, poly_ref)
-    load_variance.wait()
-
     live = count_ref[0]
-
-    def invert(b, carry):
-        flag = (b < live).astype(jnp.float32)
-        rows = pl.ds(pl.multiple_of(b * STRIP, STRIP), STRIP)
-        for chunk in range(BLOCK // STRIP):
-            core, half, step = chunk // 8, chunk // 4 % 2, chunk % 4
-            strips_ref[half * 8 + step * 2 + core, rows, :] = flag / variance_ref[b, chunk * STRIP : (chunk + 1) * STRIP, :]
-        return carry
-
-    lax.fori_loop(0, BLOCKS, invert, 0)
-    for unit in range(4):
-        slots_ref[unit] = slot_rows(patches_ref, quadrants_ref, live, unit, here)
-    pl.semaphore_wait(barrier, len(all_partners))
+    for unit in range(3):
+        ids = slot_rows(patches_ref, quadrants_ref, live, unit, here)
+        for at in range(8):
+            strips_ref[unit * 8 + at, SLAB:, :] = ids
+
+    def invert(half):
+        def step(b, carry):
+            flag = (b < live).astype(jnp.float32)
+            rows = pl.ds(pl.multiple_of(b * STRIP, STRIP), STRIP)
+            for core, step in itertools.product(range(2), range(SIDE)):
+                first = core * 64 + half * TILE + step * STRIP
+                strips_ref[half * 8 + step * 2 + core, rows, :] = flag / variance_ref[b, first : first + STRIP, :]
+            return carry
+
+        lax.fori_loop(0, BLOCKS, step, 0)
 
     def remote(src, dst, send, recv, to):
         return pltpu.make_async_remote_copy(
             src_ref=src, dst_ref=dst, send_sem=send, recv_sem=recv, device_id=to["id"], device_id_type=MESH
         )
-
-    def slots_copy(unit, o):
-        to = here.at(c=o % 2, **{UNITS[unit][2]: o // 2})
-        return remote(slots_ref.at[unit], got_slots_ref.at[unit * 8 + o], slots_send.at[unit, o], slots_recv.at[unit, o], to)
 
     def first_copy(unit, o, rows):
         axis = UNITS[unit][2]
@@ -230,16 +228,22 @@
             return pltpu.make_async_copy(source, target, first_recv.at[unit, 0])
         return remote(source, target, first_send.at[unit, o], first_recv.at[unit, o], to)
 
-    everything = pl.ds(0, SLAB)
-    for unit in range(2):
-        for o in range(8):
-            first_copy(unit, o, everything).start()
-    for unit in range(4):
-        for o in range(1, 8):
-            slots_copy(unit, o).start()
+    def all_rows(unit):
+        return pl.ds(0, SLAB if unit == 3 else FULL)
+
+    load_variance.wait()
+    invert(0)
+    pl.semaphore_wait(barrier, len(all_partners))
+    for o in range(8):
+        first_copy(0, o, all_rows(0)).start()
+    invert(1)
+    for o in range(8):
+        first_copy(1, o, all_rows(1)).start()
+    build_bands(row_ref, col_ref, left_ref, right_ref)
+    build_polynomials(table_ref, index_ref, quadrant_ref, poly_ref)
     load_image.wait()
 
-    def compute(half, every, meanwhile):
+    def compute(half, chunks, meanwhile):
         unit = 2 + half
 
         def step(group, carry):
@@ -256,25 +260,18 @@
 
                 matched_tile(core * 2 + half, first, image_ref, left_ref, right_ref, poly_ref, parts_ref, emit)
 
-            def send():
-                size = every * GROUP * STRIP
-                rows = pl.ds(pl.multiple_of(lax.div(group, every) * size, size), size)
-                for o in range(8):
-                    first_copy(unit, o, rows).start()
-
-            if every == 1:
-                send()
-            else:
-                pl.when(lax.rem(group, every) == every - 1)(send)
+            for after, begin, end in chunks:
+
+                @pl.when(group == after)
+                def send(begin=begin, end=end):
+                    for o in range(8):
+                        first_copy(unit, o, pl.ds(begin, end - begin)).start()
+
             for after, run in meanwhile:
                 pl.when(group == after)(run)
             return carry
 
         lax.fori_loop(0, BLOCKS // GROUP, step, 0)
-
-    def take_slots(unit):
-        for o in range(1, 8):
-            slots_copy(unit, o).wait_recv()
 
     def choose(own, home, away):
         if own is True:
@@ -387,14 +384,14 @@
     def gather(unit):
         for o in range(8):
             if o == 0:
-                first_copy(unit, 0, everything).wait()
+                first_copy(unit, 0, all_rows(unit)).wait()
             else:
-                first_copy(unit, o, everything).wait_recv()
-        take_slots(unit)
-        slots = slots_ref[unit]
+                first_copy(unit, o, all_rows(unit)).wait_recv()
+        ids = got_ref[unit % 3 * 8, SLAB:, :]
         for o in range(1, 8):
-            slots = jnp.maximum(slots, got_slots_ref[unit * 8 + o])
-        hot = lax.broadcasted_iota(jnp.int32, (SLOTS, 256), 0) == slots[0:1, :]
+            ids = jnp.maximum(ids, got_ref[unit % 3 * 8 + o, SLAB:, :])
+        ids = jnp.concatenate([ids[0:1, :], ids[1:2, :]], axis=1)
+        hot = lax.broadcasted_iota(jnp.int32, (SLOTS, 256), 0).astype(jnp.float32) == ids
         hot = hot.astype(jnp.float32).astype(jnp.bfloat16)
         for row in range(STRIP):
             data = jnp.concatenate(
@@ -485,8 +482,8 @@
         gather(0)
         gather(1)
 
-    compute(0, 2, ())
-    compute(1, 1, ((1, gather_inverses), (2, lambda: gather(2))))
+    compute(0, ((1, 0, SLAB // 2), (3, SLAB // 2, FULL)), ())
+    compute(1, [(g, g * SLAB // 4, (g + 1) * SLAB // 4) for g in range(4)], ((1, gather_inverses), (2, lambda: gather(2))))
     for unit in range(3):
         pass_on(unit)
     gather(3)
@@ -498,9 +495,7 @@
     finish(3)
     for unit in range(4):
         for o in range(1, 8):
-            slots_copy(unit, o).wait_send()
-        for o in range(1, 8):
-            first_copy(unit, o, everything).wait_send()
+            first_copy(unit, o, all_rows(unit)).wait_send()
         end_second(unit)
         end_third(unit)
 
@@ -524,10 +519,8 @@
             pltpu.VMEM((NB, 256, 256), bf16),
             pltpu.VMEM((BLOCKS, 3, NB, BLOCK), f32),
             pltpu.VMEM((NB, GROUP * TILE, 256), bf16),
-            pltpu.VMEM((units * 8, SLAB, BLOCK), f32),
-            pltpu.VMEM((units, 8, 256), jnp.int32),
-            pltpu.VMEM((units * 8, 8, 256), jnp.int32),
-            pltpu.VMEM((units * 8, SLAB, BLOCK), f32),
+            pltpu.VMEM((units * 8, FULL, BLOCK), f32),
+            pltpu.VMEM((units * 8, FULL, BLOCK), f32),
             pltpu.VMEM((units, STRIP, SLOTS, BLOCK), f32),
             pltpu.VMEM((units, SIDE, STRIP, 64, BLOCK), f32),
             pltpu.VMEM((units, STRIP, 64, BLOCK), f32),
@@ -535,7 +528,6 @@
             pltpu.VMEM((16, STRIP, 16, BLOCK), f32),
             pltpu.VMEM((units, 16 * STRIP, BLOCK), f32),
             pltpu.VMEM((units, SIDE, 2 * STRIP, BLOCK), f32),
-            dma((units, 8)), dma((units, 8)),
             dma((units, 8)), dma((units, 8)),
             dma((units, 16)), dma((units, 16)),
             dma((units, 8)), dma((units, SIDE)),

time: 60.1 us -> 58.8 us (0.978)
  Pallas kernels: 57.1 us -> 55.8 us
    pallas_call x1, Pallas kernels: 57.1 us -> 55.8 us  [fused(): pl.pallas_call(fused_kernel, out_shape=jax.ShapeDtypeStruct((2, 64, 256),...]
where the time goes in v5:
time: 58.8 us; the launch traced here: 58.6 us
  Pallas kernels  55.8 us (95%)
  local copies, waits for them, and re-layouts  1.53 us (3%)
  between operations  1.29 us (2%)
    pallas_call x1, Pallas kernels, fused(): pl.pallas_call(fused_kernel, out_shape=jax.ShapeDtypeStruct((2, 64, 256),...  55.8 us
    slice x1, local copies, waits for them, and re-layouts, on_device(): return (sums[1][None], sums[0][None])  1.53 us

profile of v5, /device:TPU:1, one launch (start us, length us, event | category | flops | bytes accessed | tf_op | source)
XLA Modules:
  0.0 58.6 jit_solution(11082064309390307337)
XLA Ops:
  1.3 55.8 %coadd.1 = f32[2,64,256]{2,1,0:T(8,128)} custom-call(s32[1]{0:T(128)} %bitcast.10.count_ref, s32[32]{0:T(128)} %bitcast.14, f32[32,128,128]{2,1,0:T(8,128)} %bitcast.11, f32[32,128,128]{2,1,0:T(8,128)} %bitcast.12, f32[16,41]{1,0:T(8,128)} %row_ref.1, f32[16,41]{1,0:T(8,128)} %col_ref.1, f32[96,800]{1,0:T(8,128)} %bitcast.13, s32[1,32]{1,0:T(1,128)} %bitcast.16, ...), custom_call_target="tpu_custom_call" | custom-call | tf_op jit(solution)/shard_map/coadd/pallas_call | solution.py:509
  57.1 1.5 %fusion = (f32[1,64,256]{2,1,0:T(8,128)}, f32[1,64,256]{2,1,0:T(8,128)}) fusion(f32[2,64,256]{2,1,0:T(8,128)} %coadd.1), kind=kLoop, calls=%fused_computation | loop fusion | bytes 262144 | tf_op jit(solution)/shard_map/slice | solution.py:548

commit v6 on v5

--- a/solution.py
+++ b/solution.py
@@ -22,7 +22,7 @@
 SLAB = BLOCKS * STRIP
 FULL = SLAB + STRIP
 MESH = pl.DeviceIdType.MESH
-UNITS = ((0, 0, "x", "zy"), (0, 1, "z", "yx"), (1, 0, "y", "zx"), (1, 1, "x", "plane"))
+UNITS = ((0, 0, "y", "xz"), (0, 1, "x", "zy"), (1, 0, "z", "xy"), (1, 1, "y", "plane"))
 AXES = ("x", "y", "z")
 
 
@@ -133,15 +133,25 @@
         place = lax.axis_index("patch")
         self.x, self.z, self.c = lax.div(place, 8), lax.rem(lax.div(place, 2), 4), lax.rem(place, 2)
         self.odd = lax.rem(self.y + self.c, 2)
+        self.seen = {}
 
     def strip(self, axis):
         return getattr(self, axis) * 2 + self.c
 
     def at(self, c=0, **offsets):
-        place = {axis: lax.rem(getattr(self, axis) + offsets.get(axis, 0), SIDE) for axis in AXES}
-        place["c"] = lax.rem(self.c + c, 2)
+        key = (c,) + tuple(offsets.get(axis, 0) for axis in AXES)
+        known = all(isinstance(step, int) for step in key)
+        if known and key in self.seen:
+            return dict(self.seen[key])
+        place = {
+            axis: lax.rem(getattr(self, axis) + step, SIDE) if not isinstance(step, int) or step else getattr(self, axis)
+            for axis, step in zip(AXES, key[1:])
+        }
+        place["c"] = lax.rem(self.c + c, 2) if c else self.c
         place["id"] = (place["y"], (place["x"] * SIDE + place["z"]) * 2 + place["c"])
-        return place
+        if known:
+            self.seen[key] = place
+        return dict(place)
 
 
 def partners():
@@ -190,6 +200,7 @@
     here = Here()
     barrier = pltpu.get_barrier_semaphore()
     all_partners = partners()
+    here.at()
     for x, y, z, c in all_partners:
         pl.semaphore_signal(barrier, inc=1, device_id=here.at(x=x, y=y, z=z, c=c)["id"], device_id_type=MESH)
 
@@ -198,7 +209,7 @@
     load_variance.start()
     load_image.start()
     live = count_ref[0]
-    for unit in range(3):
+    for unit in range(4):
         ids = slot_rows(patches_ref, quadrants_ref, live, unit, here)
         for at in range(8):
             strips_ref[unit * 8 + at, SLAB:, :] = ids
@@ -228,17 +239,14 @@
             return pltpu.make_async_copy(source, target, first_recv.at[unit, 0])
         return remote(source, target, first_send.at[unit, o], first_recv.at[unit, o], to)
 
-    def all_rows(unit):
-        return pl.ds(0, SLAB if unit == 3 else FULL)
-
     load_variance.wait()
     invert(0)
     pl.semaphore_wait(barrier, len(all_partners))
     for o in range(8):
-        first_copy(0, o, all_rows(0)).start()
+        first_copy(0, o, pl.ds(0, FULL)).start()
     invert(1)
     for o in range(8):
-        first_copy(1, o, all_rows(1)).start()
+        first_copy(1, o, pl.ds(0, FULL)).start()
     build_bands(row_ref, col_ref, left_ref, right_ref)
     build_polynomials(table_ref, index_ref, quadrant_ref, poly_ref)
     load_image.wait()
@@ -384,12 +392,12 @@
     def gather(unit):
         for o in range(8):
             if o == 0:
-                first_copy(unit, 0, all_rows(unit)).wait()
+                first_copy(unit, 0, pl.ds(0, FULL)).wait()
             else:
-                first_copy(unit, o, all_rows(unit)).wait_recv()
-        ids = got_ref[unit % 3 * 8, SLAB:, :]
+                first_copy(unit, o, pl.ds(0, FULL)).wait_recv()
+        ids = got_ref[unit * 8, SLAB:, :]
         for o in range(1, 8):
-            ids = jnp.maximum(ids, got_ref[unit % 3 * 8 + o, SLAB:, :])
+            ids = jnp.maximum(ids, got_ref[unit * 8 + o, SLAB:, :])
         ids = jnp.concatenate([ids[0:1, :], ids[1:2, :]], axis=1)
         hot = lax.broadcasted_iota(jnp.int32, (SLOTS, 256), 0).astype(jnp.float32) == ids
         hot = hot.astype(jnp.float32).astype(jnp.bfloat16)
@@ -483,10 +491,12 @@
         gather(1)
 
     compute(0, ((1, 0, SLAB // 2), (3, SLAB // 2, FULL)), ())
-    compute(1, [(g, g * SLAB // 4, (g + 1) * SLAB // 4) for g in range(4)], ((1, gather_inverses), (2, lambda: gather(2))))
-    for unit in range(3):
-        pass_on(unit)
+    quarters = [(g, g * SLAB // 4, (g + 1) * SLAB // 4) for g in range(3)] + [(3, SLAB * 3 // 4, FULL)]
+    compute(1, quarters, ((0, gather_inverses), (2, lambda: gather(2))))
+    pass_on(0)
+    pass_on(1)
     gather(3)
+    pass_on(2)
     for unit in range(3):
         reduce(unit)
     for unit in range(3):
@@ -495,7 +505,7 @@
     finish(3)
     for unit in range(4):
         for o in range(1, 8):
-            first_copy(unit, o, all_rows(unit)).wait_send()
+            first_copy(unit, o, pl.ds(0, FULL)).wait_send()
         end_second(unit)
         end_third(unit)
 

time: 58.8 us -> 57.5 us (0.978)
  Pallas kernels: 55.8 us -> 54.5 us
    pallas_call x1, Pallas kernels: 55.8 us -> 54.5 us  [fused(): pl.pallas_call(fused_kernel, out_shape=jax.ShapeDtypeStruct((2, 64, 256),...]
where the time goes in v6:
time: 57.5 us; the launch traced here: 57.3 us
  Pallas kernels  54.5 us (95%)
  local copies, waits for them, and re-layouts  1.53 us (3%)
  between operations  1.29 us (2%)
    pallas_call x1, Pallas kernels, fused(): pl.pallas_call(fused_kernel, out_shape=jax.ShapeDtypeStruct((2, 64, 256),...  54.5 us
    slice x1, local copies, waits for them, and re-layouts, on_device(): return (sums[1][None], sums[0][None])  1.53 us

profile of v6, /device:TPU:1, one launch (start us, length us, event | category | flops | bytes accessed | tf_op | source)
XLA Modules:
  0.0 57.3 jit_solution(13393567710672788002)
XLA Ops:
  1.3 54.5 %coadd.1 = f32[2,64,256]{2,1,0:T(8,128)} custom-call(s32[1]{0:T(128)} %bitcast.10.count_ref, s32[32]{0:T(128)} %bitcast.14, f32[32,128,128]{2,1,0:T(8,128)} %bitcast.11, f32[32,128,128]{2,1,0:T(8,128)} %bitcast.12, f32[16,41]{1,0:T(8,128)} %row_ref.1, f32[16,41]{1,0:T(8,128)} %col_ref.1, f32[96,800]{1,0:T(8,128)} %bitcast.13, s32[1,32]{1,0:T(1,128)} %bitcast.16, ...), custom_call_target="tpu_custom_call" | custom-call | tf_op jit(solution)/shard_map/coadd/pallas_call | solution.py:519
  55.8 1.5 %fusion = (f32[1,64,256]{2,1,0:T(8,128)}, f32[1,64,256]{2,1,0:T(8,128)}) fusion(f32[2,64,256]{2,1,0:T(8,128)} %coadd.1), kind=kLoop, calls=%fused_computation | loop fusion | bytes 262144 | tf_op jit(solution)/shard_map/slice | solution.py:558

commit v7 on v6

--- a/solution.py
+++ b/solution.py
@@ -197,6 +197,18 @@
     final_ref, got_final_ref,
     first_send, first_recv, second_send, second_recv, third_send, third_recv,
 ):
+    def load_half(half):
+        for core in range(2):
+            rows = pl.ds(core * 64 + half * TILE, TILE)
+            yield pltpu.make_async_copy(
+                variance_hbm.at[:, rows, :], variance_ref.at[:, rows, :], load_sem.at[1 + half * 2 + core]
+            )
+
+    load_image = pltpu.make_async_copy(image_hbm, image_ref, load_sem.at[0])
+    for half in range(2):
+        for load in load_half(half):
+            load.start()
+    load_image.start()
     here = Here()
     barrier = pltpu.get_barrier_semaphore()
     all_partners = partners()
@@ -204,10 +216,6 @@
     for x, y, z, c in all_partners:
         pl.semaphore_signal(barrier, inc=1, device_id=here.at(x=x, y=y, z=z, c=c)["id"], device_id_type=MESH)
 
-    load_variance = pltpu.make_async_copy(variance_hbm, variance_ref, load_sem.at[0])
-    load_image = pltpu.make_async_copy(image_hbm, image_ref, load_sem.at[1])
-    load_variance.start()
-    load_image.start()
     live = count_ref[0]
     for unit in range(4):
         ids = slot_rows(patches_ref, quadrants_ref, live, unit, here)
@@ -239,11 +247,14 @@
             return pltpu.make_async_copy(source, target, first_recv.at[unit, 0])
         return remote(source, target, first_send.at[unit, o], first_recv.at[unit, o], to)
 
-    load_variance.wait()
+    for load in load_half(0):
+        load.wait()
     invert(0)
     pl.semaphore_wait(barrier, len(all_partners))
     for o in range(8):
         first_copy(0, o, pl.ds(0, FULL)).start()
+    for load in load_half(1):
+        load.wait()
     invert(1)
     for o in range(8):
         first_copy(1, o, pl.ds(0, FULL)).start()
@@ -497,12 +508,10 @@
     pass_on(1)
     gather(3)
     pass_on(2)
-    for unit in range(3):
+    for unit in range(4):
         reduce(unit)
-    for unit in range(3):
+    for unit in range(4):
         finish(unit)
-    reduce(3)
-    finish(3)
     for unit in range(4):
         for o in range(1, 8):
             first_copy(unit, o, pl.ds(0, FULL)).wait_send()
@@ -524,7 +533,7 @@
         scratch_shapes=[
             pltpu.VMEM((BLOCKS, BLOCK, BLOCK), f32),
             pltpu.VMEM((BLOCKS, BLOCK, BLOCK), f32),
-            dma((2,)),
+            dma((5,)),
             pltpu.VMEM((NB * TILE, 256), bf16),
             pltpu.VMEM((NB, 256, 256), bf16),
             pltpu.VMEM((BLOCKS, 3, NB, BLOCK), f32),

time: 57.5 us -> 57.2 us (level)
  no operation moved by 1% of the time
where the time goes in v7:
time: 57.2 us; the launch traced here: 57 us
  Pallas kernels  54.2 us (95%)
  local copies, waits for them, and re-layouts  1.53 us (3%)
  between operations  1.29 us (2%)
    pallas_call x1, Pallas kernels, fused(): pl.pallas_call(fused_kernel, out_shape=jax.ShapeDtypeStruct((2, 64, 256),...  54.2 us
    slice x1, local copies, waits for them, and re-layouts, on_device(): return (sums[1][None], sums[0][None])  1.53 us

profile of v7, /device:TPU:1, one launch (start us, length us, event | category | flops | bytes accessed | tf_op | source)
XLA Modules:
  0.0 57.0 jit_solution(16701473270377655033)
XLA Ops:
  1.3 54.2 %coadd.1 = f32[2,64,256]{2,1,0:T(8,128)} custom-call(s32[1]{0:T(128)} %bitcast.10.count_ref, s32[32]{0:T(128)} %bitcast.14, f32[32,128,128]{2,1,0:T(8,128)} %bitcast.11, f32[32,128,128]{2,1,0:T(8,128)} %bitcast.12, f32[16,41]{1,0:T(8,128)} %row_ref.1, f32[16,41]{1,0:T(8,128)} %col_ref.1, f32[96,800]{1,0:T(8,128)} %bitcast.13, s32[1,32]{1,0:T(1,128)} %bitcast.16, ...), custom_call_target="tpu_custom_call" | custom-call | tf_op jit(solution)/shard_map/coadd/pallas_call | solution.py:528
  55.5 1.5 %fusion = (f32[1,64,256]{2,1,0:T(8,128)}, f32[1,64,256]{2,1,0:T(8,128)}) fusion(f32[2,64,256]{2,1,0:T(8,128)} %coadd.1), kind=kLoop, calls=%fused_computation | loop fusion | bytes 262144 | tf_op jit(solution)/shard_map/slice | solution.py:567

commit v8 on v7

--- a/solution.py
+++ b/solution.py
@@ -247,6 +247,7 @@
             return pltpu.make_async_copy(source, target, first_recv.at[unit, 0])
         return remote(source, target, first_send.at[unit, o], first_recv.at[unit, o], to)
 
+    build_bands(row_ref, col_ref, left_ref, right_ref)
     for load in load_half(0):
         load.wait()
     invert(0)
@@ -258,7 +259,6 @@
     invert(1)
     for o in range(8):
         first_copy(1, o, pl.ds(0, FULL)).start()
-    build_bands(row_ref, col_ref, left_ref, right_ref)
     build_polynomials(table_ref, index_ref, quadrant_ref, poly_ref)
     load_image.wait()
 

time: 57.2 us -> 57.1 us (level)
  no operation moved by 1% of the time
where the time goes in v8:
time: 57.1 us; the launch traced here: 56.9 us
  Pallas kernels  54.1 us (95%)
  local copies, waits for them, and re-layouts  1.53 us (3%)
  between operations  1.29 us (2%)
    pallas_call x1, Pallas kernels, fused(): pl.pallas_call(fused_kernel, out_shape=jax.ShapeDtypeStruct((2, 64, 256),...  54.1 us
    slice x1, local copies, waits for them, and re-layouts, on_device(): return (sums[1][None], sums[0][None])  1.53 us

profile of v8, /device:TPU:1, one launch (start us, length us, event | category | flops | bytes accessed | tf_op | source)
XLA Modules:
  0.0 56.9 jit_solution(9465444651483041998)
XLA Ops:
  1.3 54.1 %coadd.1 = f32[2,64,256]{2,1,0:T(8,128)} custom-call(s32[1]{0:T(128)} %bitcast.10.count_ref, s32[32]{0:T(128)} %bitcast.14, f32[32,128,128]{2,1,0:T(8,128)} %bitcast.11, f32[32,128,128]{2,1,0:T(8,128)} %bitcast.12, f32[16,41]{1,0:T(8,128)} %row_ref.1, f32[16,41]{1,0:T(8,128)} %col_ref.1, f32[96,800]{1,0:T(8,128)} %bitcast.13, s32[1,32]{1,0:T(1,128)} %bitcast.16, ...), custom_call_target="tpu_custom_call" | custom-call | tf_op jit(solution)/shard_map/coadd/pallas_call | solution.py:528
  55.4 1.5 %fusion = (f32[1,64,256]{2,1,0:T(8,128)}, f32[1,64,256]{2,1,0:T(8,128)}) fusion(f32[2,64,256]{2,1,0:T(8,128)} %coadd.1), kind=kLoop, calls=%fused_computation | loop fusion | bytes 262144 | tf_op jit(solution)/shard_map/slice | solution.py:567
